TPU v7x, 256 devices: a whole 4x4x8 slice. The times are simulated.
256 devices in a mesh: store: 32 (over y, z), tp: 8 (over x, core).
Axes of the slice: x: 4, y: 4, z: 8, core: 2. Of those that a mesh axis runs over, the one named last changes fastest.
Arguments:
- queries: bfloat16 [32768, 8192], P('store', 'tp')
- fresh_kv: bfloat16 [2, 32768, 1024], P(None, ('store', 'tp'))
- page_pool: bfloat16 [2048, 2, 128, 1024], P('store', None, None, 'tp')
- page_host: int32 [128, 8], P('store'), may hold values from 0 to 31, as said below
- page_slot: int32 [128, 8], P('store'), may hold values from 0 to 63, as said below
- prefix_len: int32 [128], P('store'), may hold values from 513 to 1024
- fresh_len: int32 [32, 4], P('store'), may hold values from 1 to 384, 1024 in all within a row
Outputs:
- attention: bfloat16 [32768, 8192], P('store', 'tp')
Inputs may be any that keep to these rules, and one draw needn't show every extreme that they name: `page_host`: page p of request r is read only if p < ceil(prefix_len[r] / 128). Among the pages read by the 4 requests of one host, at most 2 lie on any one host; in every draw some host holds exactly 2 of the pages read by each host. `page_slot`: several entries may name the same stored page. `fresh_len`: the requests of a host own consecutive rows of its block, in order.
All inputs are finite; a program needn't handle non-finite values.
Results may differ from a plain program's by a relative error of at most 0.0041.
Values may be sent and summed in bfloat16 or wider, within the bound.
A program may use at most 128 MiB of HBM per device.

v0:
```python
import math

import jax
import jax.numpy as jnp
from jax import lax
from jax.sharding import PartitionSpec as P

HD = 128
REQ_HOST = 4
PAGE = 128
PAGES_MAX = 8
MOST_NEW = 384


def plan_requests(owners, slot_ids, prefix, stores, capacity):
    entry_count = owners.shape[0] * owners.shape[1]
    page_count = (prefix + PAGE - 1) // PAGE
    in_use = (jnp.arange(owners.shape[1], dtype=jnp.int32)[None, :] < page_count[:, None]).reshape(
        entry_count
    )
    flat_owners = owners.reshape(entry_count)
    flat_slots = slot_ids.reshape(entry_count)
    entries = jnp.arange(entry_count, dtype=jnp.int32)
    same_owner = (
        (flat_owners[:, None] == flat_owners[None, :])
        & in_use[None, :]
        & (entries[None, :] < entries[:, None])
    )
    owner_rank = jnp.sum(same_owner.astype(jnp.int32), axis=1)
    position = jnp.where(in_use, flat_owners * capacity + owner_rank, 0)
    target = jnp.arange(stores * capacity, dtype=jnp.int32)
    matches = (position[:, None] == target[None, :]) & in_use[:, None]
    buffer = jnp.sum(jnp.where(matches, flat_slots[:, None], 0), axis=0)
    return (buffer.reshape(stores, capacity), position)


def attend(q_rows, key_rows, value_rows, key_valid):
    scores = jnp.einsum("mkgd,nkd->kgmn", q_rows, key_rows, preferred_element_type=jnp.float32) * (
        1.0 / math.sqrt(HD)
    )
    row_top = jnp.max(jnp.where(key_valid, scores, -1e30), axis=-1, keepdims=True)
    weights = jnp.where(key_valid, jnp.exp(scores - row_top), 0.0)
    row_total = jnp.sum(weights, axis=-1)
    rounded = weights.astype(jnp.bfloat16)
    mixed_rows = jnp.einsum(
        "kgmn,nkd->mkgd", rounded, value_rows, preferred_element_type=jnp.float32
    )
    return (mixed_rows / jnp.transpose(row_total, (2, 0, 1))[..., None]).astype(jnp.bfloat16)


def local(queries, fresh_kv, page_pool, page_host, page_slot, prefix_len, fresh_len):
    stores = lax.axis_size("store")
    block_rows = queries.shape[0]
    head_width = page_pool.shape[3]
    kv_local = head_width // HD
    group_size = queries.shape[1] // head_width
    capacity = max(2, (REQ_HOST * PAGES_MAX + stores - 1) // stores)
    gathered = lax.all_gather(fresh_kv, "tp", axis=1, tiled=True)
    new_kv = lax.dynamic_slice_in_dim(gathered, lax.axis_index("tp") * head_width, head_width, 2)
    buffer, position = plan_requests(page_host, page_slot, prefix_len, stores, capacity)
    arrived = lax.all_to_all(
        jnp.take(
            page_pool,
            lax.all_to_all(buffer, "store", split_axis=0, concat_axis=0, tiled=True),
            axis=0,
        ),
        "store",
        split_axis=0,
        concat_axis=0,
        tiled=True,
    )
    flat_pages = arrived.reshape(stores * capacity, 2, PAGE, head_width)
    fetched = jnp.take(flat_pages, position, axis=0).reshape(
        REQ_HOST, PAGES_MAX, 2, PAGE, head_width
    )
    lengths = fresh_len[0]
    offsets = jnp.cumsum(lengths) - lengths
    positions = jnp.arange(MOST_NEW, dtype=jnp.int32)
    cache_index = jnp.arange(PAGES_MAX * PAGE, dtype=jnp.int32)
    output = jnp.zeros_like(queries)
    for request in range(REQ_HOST):
        offset = offsets[request]
        length = lengths[request]
        window_start = jnp.minimum(offset, block_rows - MOST_NEW)
        q_rows = lax.dynamic_slice_in_dim(queries, window_start, MOST_NEW, 0).reshape(
            MOST_NEW, kv_local, group_size, HD
        )
        new_rows = lax.dynamic_slice_in_dim(new_kv, window_start, MOST_NEW, 1).reshape(
            2, MOST_NEW, kv_local, HD
        )
        cached_keys = fetched[request, :, 0].reshape(PAGES_MAX * PAGE, kv_local, HD)
        cached_values = fetched[request, :, 1].reshape(PAGES_MAX * PAGE, kv_local, HD)
        key_rows = jnp.concatenate([cached_keys, new_rows[0]], axis=0)
        value_rows = jnp.concatenate([cached_values, new_rows[1]], axis=0)
        query_pos = window_start + positions
        cache_ok = jnp.broadcast_to(
            cache_index[None, :] < prefix_len[request], (MOST_NEW, PAGES_MAX * PAGE)
        )
        fresh_ok = (query_pos[None, :] >= offset) & (query_pos[None, :] <= query_pos[:, None])
        key_valid = jnp.concatenate([cache_ok, fresh_ok], axis=1)
        mixed_rows = attend(q_rows, key_rows, value_rows, key_valid).reshape(
            MOST_NEW, queries.shape[1]
        )
        row_ok = (query_pos >= offset) & (query_pos < offset + length)
        old_rows = lax.dynamic_slice_in_dim(output, window_start, MOST_NEW, 0)
        output = lax.dynamic_update_slice_in_dim(
            output, jnp.where(row_ok[:, None], mixed_rows, old_rows), window_start, 0
        )
    return output


def solution(mesh):
    placed = (
        P("store", "tp"),
        P(None, ("store", "tp"), None),
        P("store", None, None, "tp"),
        P("store", None),
        P("store", None),
        P("store"),
        P("store", None),
    )
    return jax.shard_map(
        local, mesh=mesh, in_specs=placed, out_specs=P("store", "tp"), check_vma=False
    )
```

profile of v0, /device:TPU:40, one launch (start us, length us, event | category | flops | bytes accessed | tf_op | source)
XLA Modules:
  0.0 309.6 jit_solution(1080985737066531450)
XLA Ops:
  6.5 0.8 and_select_fusion
  7.5 0.8 reshape.415
  8.5 0.8 broadcast_in_dim.157
  9.4 18.8 %all_to_all.20 = s32[32,1,2]{2,1,0:T(1,128)S(1)} all-to-all(s32[32,1,2]{2,1,0:T(1,128)S(1)} %bitcast.273), channel_id=1, replica_groups=mesh['store'=32,'tp'=8] {'store'}, dimensions={0} | all-to-all | bytes 512 | tf_op jit(solution)/shard_map/all_to_all | solution.py:64
  28.7 5.3 %gather_fusion = bf16[64,2,128,128]{3,2,1,0:T(8,128)(2,1)} fusion(bf16[64,2,128,128]{3,2,1,0:T(8,128)(2,1)} %param.9, s32[1024]{0:T(1024)S(1)} %pad_clamp_fusion.1), kind=kCustom, calls=%fused_computation | custom fusion | bytes 8388864 | tf_op jit(solution)/shard_map/jit(_take)/gather | solution.py:62
  33.9 4.5 %broadcast_select_fusion = bf16[32,2,2,128,128]{4,3,2,1,0:T(8,128)(2,1)} fusion(bf16[32,2,2,128,128]{4,3,2,1,0:T(8,128)(2,1)} %bitcast.255, pred[32,2]{1,0:T(8,128)(4,1)S(1)} %copy.87), kind=kLoop, calls=%fused_computation.42 | loop fusion | flops 2097152 | bytes 8388672 | tf_op jit(solution)/shard_map/jit(_take)/select_n | solution.py:62
  38.5 6.7 %all-to-all-start.1 = ((bf16[32,2,2,128,128]{4,3,2,1,0:T(8,128)(2,1)}), bf16[32,2,2,128,128]{4,3,2,1,0:T(8,128)(2,1)}, u32[]{:S(2)}, u32[]{:S(2)}) async-start(bf16[32,2,2,128,128]{4,3,2,1,0:T(8,128)(2,1)} %broadcast_select_fusion), calls=%async_computation.1 | async-start | bytes 8388608 | tf_op jit(solution)/shard_map/all_to_all | solution.py:61
  49.4 2.1 constant_dynamic-slice_fusion
  51.5 2.3 copy.129
  55.9 2.4 copy.128
  61.5 1.2 copy.127
  64.3 1.5 copy.126
  72.3 11.4 %all-gather.2.cloned.1.call-done = bf16[2,1024,1024]{2,1,0:T(8,128)(2,1)} async-done(((bf16[2,128,1024]{2,1,0:T(8,128)(2,1)}), bf16[2,1024,1024]{2,1,0:T(8,128)(2,1)}) %all-gather.2.cloned.1.call-update) | async-done | bytes 4194320 | tf_op jit(solution)/shard_map/all_gather | solution.py:58
  83.7 2.8 dynamic-slice_bitcast_fusion.1
  86.5 0.7 copy.109
  87.2 0.8 copy.103
  88.0 0.7 copy.97
  88.7 0.8 copy.91
  89.5 50.2 %all-to-all-done.1 = bf16[32,2,2,128,128]{4,3,2,1,0:T(8,128)(2,1)} async-done(((bf16[32,2,2,128,128]{4,3,2,1,0:T(8,128)(2,1)}), bf16[32,2,2,128,128]{4,3,2,1,0:T(8,128)(2,1)}, u32[]{:S(2)}, u32[]{:S(2)}) %all-to-all-start.1) | async-done | bytes 4194336 | tf_op jit(solution)/shard_map/all_to_all | solution.py:61
  139.7 4.3 %gather_fusion.1 = bf16[32,2,128,128]{3,2,1,0:T(8,128)(2,1)} fusion(bf16[64,2,128,128]{3,2,1,0:T(8,128)(2,1)} %bitcast.9, s32[1024]{0:T(1024)S(1)} %pad_clamp_fusion), kind=kCustom, calls=%fused_computation.1 | custom fusion | bytes 4194432 | tf_op jit(solution)/shard_map/jit(_take)/gather | solution.py:73
  144.0 1.8 broadcast_select_fusion.1
  145.8 1.2 fusion.92
  147.0 1.8 copy.125
  148.8 9.9 %fusion = (f32[8,384]{1,0:T(8,128)S(1)}, f32[1408,384,8]{1,0,2:T(8,128)}) fusion(pred[384,1408]{0,1:T(8,128)(4,1)S(1)} %pad_add_fusion.3, bf16[384,8,128]{0,2,1:T(8,128)(2,1)} %bitcast.260, bf16[384,1,128]{2,0,1:T(8,128)(2,1)} %get-tuple-element.9, bf16[1024,1,128]{2,0,1:T(8,128)(2,1)} %bitcast.264), kind=kOutput, calls=%fused_computation.4 | convolution fusion | flops 1120990208 | bytes 19001344 | tf_op jit(solution)/shard_map/mkgd,nkd->kgmn/dot_general | solution.py:38
  158.7 9.8 %fusion.18 = f32[8,384]{1,0:T(8,128)S(1)} fusion(f32[1408,384,8]{1,0,2:T(8,128)} %get-tuple-element.44, f32[8,384]{1,0:T(8,128)S(1)} %get-tuple-element.43, pred[384,1408]{0,1:T(8,128)(4,1)S(1)} %pad_add_fusion.3), kind=kLoop, calls=%fused_computation.28 | loop fusion | flops 17298432 | bytes 17866752 | tf_op jit(solution)/shard_map/reduce_sum | solution.py:43
  168.5 10.7 %fusion.36 = bf16[384,1,8,128]{0,3,2,1:T(8,128)(2,1)} fusion(f32[1408,384,8]{1,0,2:T(8,128)} %get-tuple-element.44, f32[8,384]{1,0:T(8,128)S(1)} %get-tuple-element.43, pred[384,1408]{0,1:T(8,128)(4,1)S(1)} %pad_add_fusion.3, f32[384,8]{0,1:T(8,128)S(1)} %bitcast.274, bf16[384,1,128]{0,2,1:T(8,128)(2,1)} %copy.109, bf16[1024,1,128]{0,2,1:T(8,128)(2,1)} %copy.125), kind=kOutput, calls=%fused_computation.49 | convolution fusion | flops 1126105088 | bytes 19013632 | tf_op jit(solution)/shard_map/kgmn,nkd->mkgd/dot_general | solution.py:45
  179.2 2.3 copy.113
  181.5 1.8 copy.124
  183.3 9.9 %fusion.3 = (f32[8,384]{1,0:T(8,128)S(1)}, f32[1408,384,8]{1,0,2:T(8,128)}) fusion(pred[384,1408]{0,1:T(8,128)(4,1)S(1)} %pad_add_fusion.2, bf16[384,8,128]{0,2,1:T(8,128)(2,1)} %bitcast.259, bf16[384,1,128]{2,0,1:T(8,128)(2,1)} %get-tuple-element.10, bf16[1024,1,128]{2,0,1:T(8,128)(2,1)} %bitcast.263), kind=kOutput, calls=%fused_computation.9 | convolution fusion | flops 1120990208 | bytes 19001344 | tf_op jit(solution)/shard_map/mkgd,nkd->kgmn/dot_general | solution.py:38
  193.3 9.4 %fusion.16 = f32[8,384]{1,0:T(8,128)S(1)} fusion(f32[1408,384,8]{1,0,2:T(8,128)} %get-tuple-element.42, f32[8,384]{1,0:T(8,128)S(1)} %get-tuple-element.41, pred[384,1408]{0,1:T(8,128)(4,1)S(1)} %pad_add_fusion.2), kind=kLoop, calls=%fused_computation.26 | loop fusion | flops 17298432 | bytes 17866752 | tf_op jit(solution)/shard_map/reduce_sum | solution.py:43
  202.7 10.8 %fusion.37 = bf16[384,1,8,128]{0,3,2,1:T(8,128)(2,1)} fusion(f32[1408,384,8]{1,0,2:T(8,128)} %get-tuple-element.42, f32[8,384]{1,0:T(8,128)S(1)} %get-tuple-element.41, pred[384,1408]{0,1:T(8,128)(4,1)S(1)} %pad_add_fusion.2, f32[384,8]{0,1:T(8,128)S(1)} %bitcast.275, bf16[384,1,128]{0,2,1:T(8,128)(2,1)S(1)} %copy-done.9, bf16[1024,1,128]{0,2,1:T(8,128)(2,1)} %copy.124), kind=kOutput, calls=%fused_computation.51 | convolution fusion | flops 1126105088 | bytes 19013632 | tf_op jit(solution)/shard_map/kgmn,nkd->mkgd/dot_general | solution.py:45
  213.5 2.3 copy.107
  215.9 0.8 copy.123
  216.7 8.9 %fusion.6 = (f32[8,384]{1,0:T(8,128)S(1)}, f32[1408,384,8]{1,0,2:T(8,128)}) fusion(pred[384,1408]{0,1:T(8,128)(4,1)S(1)} %pad_add_fusion.1, bf16[384,8,128]{0,2,1:T(8,128)(2,1)} %bitcast.258, bf16[384,1,128]{2,0,1:T(8,128)(2,1)S(1)} %copy-done.6, bf16[1024,1,128]{2,0,1:T(8,128)(2,1)S(1)} %bitcast.262), kind=kOutput, calls=%fused_computation.14 | convolution fusion | flops 1120990208 | bytes 19001344 | tf_op jit(solution)/shard_map/mkgd,nkd->kgmn/dot_general | solution.py:38
  225.6 9.5 %fusion.14 = f32[8,384]{1,0:T(8,128)S(1)} fusion(f32[1408,384,8]{1,0,2:T(8,128)} %get-tuple-element.40, f32[8,384]{1,0:T(8,128)S(1)} %get-tuple-element.39, pred[384,1408]{0,1:T(8,128)(4,1)S(1)} %pad_add_fusion.1), kind=kLoop, calls=%fused_computation.24 | loop fusion | flops 17298432 | bytes 17866752 | tf_op jit(solution)/shard_map/reduce_sum | solution.py:43
  235.1 9.7 %fusion.38 = bf16[384,1,8,128]{0,3,2,1:T(8,128)(2,1)S(1)} fusion(f32[1408,384,8]{1,0,2:T(8,128)} %get-tuple-element.40, f32[8,384]{1,0:T(8,128)S(1)} %get-tuple-element.39, pred[384,1408]{0,1:T(8,128)(4,1)S(1)} %pad_add_fusion.1, f32[384,8]{0,1:T(8,128)S(1)} %bitcast.276, bf16[384,1,128]{0,2,1:T(8,128)(2,1)S(1)} %copy-done.8, bf16[1024,1,128]{0,2,1:T(8,128)(2,1)} %copy.123), kind=kOutput, calls=%fused_computation.53 | convolution fusion | flops 1126105088 | bytes 19013632 | tf_op jit(solution)/shard_map/kgmn,nkd->mkgd/dot_general | solution.py:45
  244.8 1.2 copy.101
  246.2 7.9 %fusion.9 = (f32[8,384]{1,0:T(8,128)S(1)}, f32[1408,384,8]{1,0,2:T(8,128)}) fusion(pred[384,1408]{0,1:T(8,128)(4,1)S(1)} %pad_add_fusion, bf16[384,8,128]{0,2,1:T(8,128)(2,1)S(1)} %bitcast.257, bf16[384,1,128]{2,0,1:T(8,128)(2,1)S(1)} %copy-done.5, bf16[1024,1,128]{2,0,1:T(8,128)(2,1)S(1)} %bitcast.261), kind=kOutput, calls=%fused_computation.19 | convolution fusion | flops 1120990208 | bytes 19001344 | tf_op jit(solution)/shard_map/mkgd,nkd->kgmn/dot_general | solution.py:38
  254.1 9.4 %fusion.12 = f32[8,384]{1,0:T(8,128)S(1)} fusion(f32[1408,384,8]{1,0,2:T(8,128)} %get-tuple-element.38, f32[8,384]{1,0:T(8,128)S(1)} %get-tuple-element.37, pred[384,1408]{0,1:T(8,128)(4,1)S(1)} %pad_add_fusion), kind=kLoop, calls=%fused_computation.22 | loop fusion | flops 17298432 | bytes 17866752 | tf_op jit(solution)/shard_map/reduce_sum | solution.py:43
  263.6 9.7 %fusion.39 = bf16[384,1,8,128]{0,3,2,1:T(8,128)(2,1)S(1)} fusion(f32[1408,384,8]{1,0,2:T(8,128)} %get-tuple-element.38, f32[8,384]{1,0:T(8,128)S(1)} %get-tuple-element.37, pred[384,1408]{0,1:T(8,128)(4,1)S(1)} %pad_add_fusion, f32[384,8]{0,1:T(8,128)S(1)} %bitcast.277, bf16[384,1,128]{0,2,1:T(8,128)(2,1)S(1)} %copy-done.7, bf16[1024,1,128]{0,2,1:T(8,128)(2,1)S(1)} %copy.122), kind=kOutput, calls=%fused_computation.55 | convolution fusion | flops 1126105088 | bytes 19013632 | tf_op jit(solution)/shard_map/kgmn,nkd->mkgd/dot_general | solution.py:45
  273.5 1.0 broadcast_select_fusion.2
  274.8 5.6 %dynamic_update_slice.12 = bf16[1024,1024]{1,0:T(8,128)(2,1)S(1)} dynamic-update-slice(bf16[1024,1024]{1,0:T(8,128)(2,1)S(1)} %broadcast_in_dim.152, bf16[384,1024]{1,0:T(8,128)(2,1)} %broadcast_select_fusion.2, s32[]{:T(128)S(6)} %select_n.157, s32[]{:T(128)} %constant.116.clone.1) | dynamic-update-slice | bytes 1572868 | tf_op jit(solution)/shard_map/dynamic_update_slice | solution.py:106
  280.4 2.3 dynamic-slice_select_fusion.2
  282.8 5.5 %dynamic_update_slice.13 = bf16[1024,1024]{1,0:T(8,128)(2,1)S(1)} dynamic-update-slice(bf16[1024,1024]{1,0:T(8,128)(2,1)S(1)} %dynamic_update_slice.12, bf16[384,1024]{1,0:T(8,128)(2,1)} %dynamic-slice_select_fusion.2, s32[]{:T(128)S(6)} %select_n.164, s32[]{:T(128)} %constant.116.clone.1) | dynamic-update-slice | bytes 1572868 | tf_op jit(solution)/shard_map/dynamic_update_slice | solution.py:106
  288.3 2.3 dynamic-slice_select_fusion.1
  290.7 5.5 %dynamic_update_slice.14 = bf16[1024,1024]{1,0:T(8,128)(2,1)S(1)} dynamic-update-slice(bf16[1024,1024]{1,0:T(8,128)(2,1)S(1)} %dynamic_update_slice.13, bf16[384,1024]{1,0:T(8,128)(2,1)} %dynamic-slice_select_fusion.1, s32[]{:T(128)S(6)} %select_n.169, s32[]{:T(128)} %constant.116.clone.1) | dynamic-update-slice | bytes 1572868 | tf_op jit(solution)/shard_map/dynamic_update_slice | solution.py:106
  296.2 1.5 dynamic-slice_select_fusion
  297.8 4.7 %dynamic_update_slice.15 = bf16[1024,1024]{1,0:T(8,128)(2,1)} dynamic-update-slice(bf16[1024,1024]{1,0:T(8,128)(2,1)} %copy-done, bf16[384,1024]{1,0:T(8,128)(2,1)} %dynamic-slice_select_fusion, s32[]{:T(128)S(6)} %select_n.174, s32[]{:T(128)} %constant.116.clone.1) | dynamic-update-slice | bytes 1572868 | tf_op jit(solution)/shard_map/dynamic_update_slice | solution.py:106
  (80 shorter events, 11.8 us)
Async XLA Ops:
  6.5 47.3 %copy-start.10 = (s32[4,8]{1,0:T(4,128)S(1)}, s32[4,8]{1,0:T(4,128)}, u32[]{:S(2)}) copy-start(s32[4,8]{1,0:T(4,128)} %param.10) | copy-start | bytes 388
  6.5 39.4 %copy-start.11 = (s32[1,4]{1,0:T(1,128)S(1)}, s32[1,4]{1,0:T(1,128)}, u32[]{:S(2)}) copy-start(s32[1,4]{1,0:T(1,128)} %param.13) | copy-start | bytes 52
  6.5 42.9 %copy-start.1 = (bf16[1024,1024]{1,0:T(8,128)(2,1)S(1)}, bf16[1024,1024]{1,0:T(8,128)(2,1)}, u32[]{:S(2)}) copy-start(bf16[1024,1024]{1,0:T(8,128)(2,1)} %param.7) | copy-start | bytes 6291460
  28.7 30.8 %copy-start.12 = (s32[4]{0:T(128)S(1)}, s32[4]{0:T(128)}, u32[]{:S(2)}) copy-start(s32[4]{0:T(128)} %param.12) | copy-start | bytes 52
  38.5 101.2 %all-to-all-start.1 = ((bf16[32,2,2,128,128]{4,3,2,1,0:T(8,128)(2,1)}), bf16[32,2,2,128,128]{4,3,2,1,0:T(8,128)(2,1)}, u32[]{:S(2)}, u32[]{:S(2)}) async-start(bf16[32,2,2,128,128]{4,3,2,1,0:T(8,128)(2,1)} %broadcast_select_fusion), calls=%async_computation.1 | async-start | bytes 8388608 | tf_op jit(solution)/shard_map/all_to_all | solution.py:61
  45.2 38.5 %all-gather.2.cloned.1.call-start = ((), (), s32[]{:S(2)}) async-start(), calls=%async_computation.2 | async-start | bytes 4718592 | tf_op jit(solution)/shard_map/all_gather | solution.py:58
  183.3 19.4 %copy-start.9 = (bf16[384,1,128]{0,2,1:T(8,128)(2,1)S(1)}, bf16[384,1,128]{0,2,1:T(8,128)(2,1)}, u32[]{:S(2)}) copy-start(bf16[384,1,128]{0,2,1:T(8,128)(2,1)} %copy.103) | copy-start | bytes 294916
  202.7 13.2 %copy-start.4 = (bf16[1,8,1,128,128]{4,3,2,1,0:T(8,128)(2,1)S(1)}, bf16[1,8,1,128,128]{4,3,2,1,0:T(8,128)(2,1)}, u32[]{:S(2)}) copy-start(bf16[1,8,1,128,128]{4,3,2,1,0:T(8,128)(2,1)} %get-tuple-element.18) | copy-start | bytes 786436
  202.7 14.0 %copy-start.6 = (bf16[384,1,128]{2,0,1:T(8,128)(2,1)S(1)}, bf16[384,1,128]{2,0,1:T(8,128)(2,1)}, u32[]{:S(2)}) copy-start(bf16[384,1,128]{2,0,1:T(8,128)(2,1)} %get-tuple-element.11) | copy-start | bytes 294916
  225.6 9.5 %copy-start.8 = (bf16[384,1,128]{0,2,1:T(8,128)(2,1)S(1)}, bf16[384,1,128]{0,2,1:T(8,128)(2,1)}, u32[]{:S(2)}) copy-start(bf16[384,1,128]{0,2,1:T(8,128)(2,1)} %copy.97) | copy-start | bytes 294916
  235.0 11.0 %copy-start.3 = (bf16[1,8,1,128,128]{4,3,2,1,0:T(8,128)(2,1)S(1)}, bf16[1,8,1,128,128]{4,3,2,1,0:T(8,128)(2,1)}, u32[]{:S(2)}) copy-start(bf16[1,8,1,128,128]{4,3,2,1,0:T(8,128)(2,1)} %get-tuple-element.20) | copy-start | bytes 786436
  235.0 11.1 %copy-start.5 = (bf16[384,1,128]{2,0,1:T(8,128)(2,1)S(1)}, bf16[384,1,128]{2,0,1:T(8,128)(2,1)}, u32[]{:S(2)}) copy-start(bf16[384,1,128]{2,0,1:T(8,128)(2,1)} %get-tuple-element.12) | copy-start | bytes 294916
  246.2 17.4 %copy-start.7 = (bf16[384,1,128]{0,2,1:T(8,128)(2,1)S(1)}, bf16[384,1,128]{0,2,1:T(8,128)(2,1)}, u32[]{:S(2)}) copy-start(bf16[384,1,128]{0,2,1:T(8,128)(2,1)} %copy.91) | copy-start | bytes 294916
  263.6 32.7 %copy-start.2 = (bf16[384,1024]{1,0:T(8,128)(2,1)S(1)}, bf16[384,1024]{1,0:T(8,128)(2,1)}, u32[]{:S(2)}) copy-start(bf16[384,1024]{1,0:T(8,128)(2,1)} %copy.113) | copy-start | bytes 2359300
  296.2 1.6 copy-start
Sparse Core Ops, SparseCore 0:
  47.9 35.7 all-gather.1
where the time goes:
time: 315 us; the launch traced here: 310 us
  matrix products  77.5 us (25%)
  local copies, waits for them, and re-layouts  62.7 us (20%)
  waiting for transfers between devices  62.1 us (20%)
  other arithmetic  60 us (19%)
  between operations  21.5 us (7%)
  blocking collectives  18.8 us (6%)
  starting transfers between devices  6.96 us (2%)
    all_to_all x1, waiting for transfers between devices, local(): lax.all_to_all(jnp.take(page_pool, lax.all_to_all(buffer, 'store', split_...  50.2 us
    dot_general x4, matrix products, attend(): jnp.einsum('kgmn,nkd->mkgd', rounded, value_rows, preferred_element_type=...  40.9 us
    reduce_sum x4, other arithmetic, attend(): row_total = jnp.sum(weights, axis=-1)  38.1 us
    dot_general x4, matrix products, attend(): jnp.einsum('mkgd,nkd->kgmn', q_rows, key_rows, preferred_element_type=jnp...  36.7 us
    dynamic_update_slice x4, local copies, waits for them, and re-layouts, local(): lax.dynamic_update_slice_in_dim(output, jnp.where(row_ok[:, None], mixed_...  21.4 us
    all_to_all x1, blocking collectives, local(): lax.all_to_all(buffer, 'store', split_axis=0, concat_axis=0, tiled=True)  18.8 us
    all_gather x1, waiting for transfers between devices, local(): gathered = lax.all_gather(fresh_kv, 'tp', axis=1, tiled=True)  11.4 us
    unnamed x30, local copies, waits for them, and re-layouts  7.46 us
  transfers between devices with their start and end apart: 2, of which 2 were waited for; matrix products, arithmetic and copies ran while one was open for 8% of the time, Pallas kernels for 0%

commit v1 on v0

v1 whole, which is shorter than its diff:
```python
import functools
import math

import jax
import jax.numpy as jnp
from jax import lax
from jax.experimental import pallas as pl
from jax.experimental.pallas import tpu as pltpu
from jax.sharding import PartitionSpec as P

HD = 128
PAGE = 128
CAP = 2
NEG = -1e30
MESH = pl.DeviceIdType.MESH
LANES = 128


def exchange_kernel(
    stores, tps, codes_ref, fresh_ref, pool_ref, arrived_ref, new_ref,
    want, got, got_s, pool_v, send_v,
    local_sem, want_send, want_recv, page_send, page_recv, new_send, new_recv,
):
    me = lax.axis_index("store")
    mt = lax.axis_index("tp")
    slots = pool_v.shape[0]
    rows = fresh_ref.shape[1]

    pool_copy = pltpu.make_async_copy(pool_ref, pool_v, local_sem.at[0])
    pool_copy.start()
    own_new = pltpu.make_async_copy(
        fresh_ref.at[:, :, pl.ds(pl.multiple_of(mt * HD, HD), HD)],
        new_ref.at[:, pl.ds(pl.multiple_of(mt * rows, rows), rows), :],
        local_sem.at[1],
    )
    own_new.start()

    barrier = pltpu.get_barrier_semaphore()

    def greet_store(i, c):
        d = lax.rem(me + i, stores)
        pl.semaphore_signal(barrier, inc=1, device_id={"store": d}, device_id_type=MESH)
        return c

    def greet_tp(i, c):
        d = lax.rem(mt + i, tps)
        pl.semaphore_signal(barrier, inc=1, device_id={"tp": d}, device_id_type=MESH)
        return c

    lax.fori_loop(1, stores, greet_store, 0)
    lax.fori_loop(1, tps, greet_tp, 0)

    codes = codes_ref[0:1, :]
    owner = lax.shift_right_arithmetic(codes, 12)
    item = jnp.bitwise_and(codes, 4095)
    source = lax.broadcasted_iota(jnp.int32, (stores, LANES), 0)
    lane = lax.broadcasted_iota(jnp.int32, (stores, LANES), 1)
    match = jnp.broadcast_to(owner, (stores, LANES)) == source
    item = jnp.broadcast_to(item, (stores, LANES))
    first = jnp.min(jnp.where(match, item, 4095), axis=1, keepdims=True)
    second = jnp.max(jnp.where(match, item, 0), axis=1, keepdims=True)
    both = jnp.where(lane == 0, first, second)
    want[...] = jnp.bitwise_and(both, slots - 1).reshape(stores, 1, LANES)

    pl.semaphore_wait(barrier, stores - 1 + tps - 1)

    def new_copy(i):
        d = lax.rem(mt + i, tps)
        return pltpu.make_async_remote_copy(
            src_ref=fresh_ref.at[:, :, pl.ds(pl.multiple_of(d * HD, HD), HD)],
            dst_ref=new_ref.at[:, pl.ds(pl.multiple_of(mt * rows, rows), rows), :],
            send_sem=new_send.at[i],
            recv_sem=new_recv.at[i],
            device_id={"tp": d},
            device_id_type=MESH,
        )

    def want_copy(i):
        d = lax.rem(me + i, stores)
        return pltpu.make_async_remote_copy(
            src_ref=want.at[d],
            dst_ref=got.at[me],
            send_sem=want_send.at[i],
            recv_sem=want_recv.at[i],
            device_id={"store": d},
            device_id_type=MESH,
        )

    def page_copy(i):
        d = lax.rem(me + i, stores)
        return pltpu.make_async_remote_copy(
            src_ref=send_v.at[d],
            dst_ref=arrived_ref.at[me],
            send_sem=page_send.at[i],
            recv_sem=page_recv.at[i],
            device_id={"store": d},
            device_id_type=MESH,
        )

    def run(start, stop, body):
        def step(i, c):
            body(i)
            return c
        lax.fori_loop(start, stop, step, 0)

    run(1, stores, lambda i: want_copy(i).start())
    run(1, tps, lambda i: new_copy(i).start())
    got_own = pltpu.make_async_copy(want.at[me], got.at[me], local_sem.at[2])
    got_own.start()
    got_own.wait()
    run(1, stores, lambda i: want_copy(i).wait())
    scalars = pltpu.make_async_copy(got, got_s, local_sem.at[3])
    scalars.start()
    pool_copy.wait()
    scalars.wait()

    def pack(i):
        d = lax.rem(me + i, stores)
        send_v[d, 0] = pool_v[got_s[d, 0, 0]]
        send_v[d, 1] = pool_v[got_s[d, 0, 1]]

    def pack_send(i):
        pack(i)
        page_copy(i).start()

    run(1, stores, pack_send)
    pack(0)
    own = pltpu.make_async_copy(send_v.at[me], arrived_ref.at[me], local_sem.at[4])
    own.start()
    own.wait()
    own_new.wait()
    run(1, tps, lambda i: new_copy(i).wait())
    run(1, stores, lambda i: page_copy(i).wait())


def exchange(codes, fresh_kv, page_pool, stores, tps):
    slots, _, page, width = page_pool.shape
    rows = fresh_kv.shape[1]
    dt = page_pool.dtype
    any_spec = pl.BlockSpec(memory_space=pl.ANY)
    return pl.pallas_call(
        functools.partial(exchange_kernel, stores, tps),
        out_shape=(
            jax.ShapeDtypeStruct((stores, CAP, 2, page, width), dt),
            jax.ShapeDtypeStruct((2, rows * tps, HD), dt),
        ),
        in_specs=[pl.BlockSpec(memory_space=pltpu.VMEM), any_spec, any_spec],
        out_specs=(any_spec, any_spec),
        scratch_shapes=[
            pltpu.VMEM((stores, 1, LANES), jnp.int32),
            pltpu.VMEM((stores, 1, LANES), jnp.int32),
            pltpu.SMEM((stores, 1, LANES), jnp.int32),
            pltpu.VMEM((slots, 2, page, width), dt),
            pltpu.VMEM((stores, CAP, 2, page, width), dt),
            pltpu.SemaphoreType.DMA((5,)),
            pltpu.SemaphoreType.DMA((stores,)),
            pltpu.SemaphoreType.DMA((stores,)),
            pltpu.SemaphoreType.DMA((stores,)),
            pltpu.SemaphoreType.DMA((stores,)),
            pltpu.SemaphoreType.DMA((tps,)),
            pltpu.SemaphoreType.DMA((tps,)),
        ],
        compiler_params=pltpu.CompilerParams(
            collective_id=0, has_side_effects=True, vmem_limit_bytes=24 << 20
        ),
        name="exchange",
    )(codes, fresh_kv, page_pool)


ROWS = 64
KEYS = 256


def attend_kernel(
    heads, host_s, slot_s, prefix_s, length_s, q_ref, new_ref, arrived_ref, out_ref,
    kv, fresh, scores, top, acc, count, page_sem, new_sem,
):
    requests, pages = host_s.shape
    stores = count.shape[0]
    block_rows = q_ref.shape[0]
    scale = math.log2(math.e) / math.sqrt(HD)
    stack = ROWS * heads

    new_copy = pltpu.make_async_copy(new_ref, fresh, new_sem)
    new_copy.start()

    def clear(i, c):
        count[i] = 0
        return c

    lax.fori_loop(0, stores, clear, 0)

    def page_copies(r, p, at):
        return [
            pltpu.make_async_copy(
                arrived_ref.at[at, half],
                kv.at[r, half, pl.ds(pl.multiple_of(p * PAGE, PAGE), PAGE), :],
                page_sem.at[r, p, half],
            )
            for half in range(2)
        ]

    for r in range(requests):
        used = lax.div(prefix_s[r] + (PAGE - 1), PAGE)

        def fetch(p, last):
            host = host_s[r, p]
            rank = count[host]
            count[host] = jnp.where(p < used, rank + 1, rank)
            at = jnp.where(p < used, host * CAP + jnp.minimum(rank, CAP - 1), last)
            for copy in page_copies(r, p, at):
                copy.start()
            return at

        lax.fori_loop(0, pages, fetch, 0)

    new_copy.wait()
    key_lane = lax.broadcasted_iota(jnp.int32, (stack, KEYS), 1)
    row_in_block = lax.rem(lax.broadcasted_iota(jnp.int32, (stack, KEYS), 0), ROWS)
    ones = jnp.ones((KEYS, HD), jnp.bfloat16)
    out_row = lax.broadcasted_iota(jnp.int32, (ROWS, HD), 0)

    def one_request(r, offset):
        length = length_s[0, r]
        prefix = prefix_s[r]

        def wait_page(p, c):
            for copy in page_copies(r, p, 0):
                copy.wait()
            return c

        lax.fori_loop(0, pages, wait_page, 0)
        chunks = lax.div(prefix + (KEYS - 1), KEYS)

        def one_block(b, c):
            row0 = pl.multiple_of(b * ROWS, ROWS)
            q = q_ref[pl.ds(row0, ROWS), :]
            q = jnp.concatenate([q[:, h * HD:(h + 1) * HD] for h in range(heads)], axis=0)
            top[...] = jnp.full((stack, HD), NEG, jnp.float32)

            def note(s, at):
                scores[at] = s
                top[...] = jnp.maximum(top[...], jnp.maximum(s[:, :HD], s[:, HD:]))

            def dot(k):
                return lax.dot_general(
                    q, k, (((1,), (1,)), ((), ())), preferred_element_type=jnp.float32
                )

            def cached(i, c):
                note(dot(kv[r, 0, pl.ds(pl.multiple_of(i * KEYS, KEYS), KEYS), :]), i)
                return c

            lax.fori_loop(0, chunks - 1, cached, 0)
            last = chunks - 1
            s = dot(kv[r, 0, pl.ds(pl.multiple_of(last * KEYS, KEYS), KEYS), :])
            note(jnp.where(key_lane < prefix - last * KEYS, s, NEG), last)

            f0 = lax.div(offset, KEYS)
            f1 = lax.div(row0 + (ROWS - 1), KEYS) + 1

            def new_keys(i, c):
                s = dot(fresh[0, pl.ds(pl.multiple_of(i * KEYS, KEYS), KEYS), :])
                key = key_lane + i * KEYS
                ok = (key >= offset) & (key <= row_in_block + row0)
                note(jnp.where(ok, s, NEG), chunks + i - f0)
                return c

            lax.fori_loop(f0, f1, new_keys, 0)
            m = jnp.max(top[...], axis=1, keepdims=True) * scale
            acc[...] = jnp.zeros((stack, 2 * HD), jnp.float32)

            def mix(at, v):
                w = jnp.exp2(scores[at] * scale - m).astype(jnp.bfloat16)
                v = jnp.concatenate([v, ones], axis=1)
                acc[...] += jnp.dot(w, v, preferred_element_type=jnp.float32)

            def cached_mix(i, c):
                mix(i, kv[r, 1, pl.ds(pl.multiple_of(i * KEYS, KEYS), KEYS), :])
                return c

            lax.fori_loop(0, chunks, cached_mix, 0)

            def new_mix(i, c):
                mix(chunks + i - f0, fresh[1, pl.ds(pl.multiple_of(i * KEYS, KEYS), KEYS), :])
                return c

            lax.fori_loop(f0, f1, new_mix, 0)
            mine = (out_row + row0 >= offset) & (out_row + row0 < offset + length)
            for h in range(heads):
                a = acc[h * ROWS:(h + 1) * ROWS, :]
                o = (a[:, :HD] / a[:, HD:]).astype(jnp.bfloat16)
                old = out_ref[pl.ds(row0, ROWS), h * HD:(h + 1) * HD]
                out_ref[pl.ds(row0, ROWS), h * HD:(h + 1) * HD] = jnp.where(mine, o, old)
            return c

        lax.fori_loop(lax.div(offset, ROWS), lax.div(offset + length - 1, ROWS) + 1, one_block, 0)
        return offset + length

    lax.fori_loop(0, requests, one_request, 0)


def attention(queries, new_kv, arrived, page_host, page_slot, prefix_len, fresh_len):
    block_rows, width = queries.shape
    requests, pages = page_host.shape
    heads = width // HD
    stores = arrived.shape[0]
    stack = ROWS * heads
    keys = pages * PAGE
    smem = pl.BlockSpec(memory_space=pltpu.SMEM)
    any_spec = pl.BlockSpec(memory_space=pl.ANY)
    vmem = pl.BlockSpec(memory_space=pltpu.VMEM)
    flat = arrived.reshape(stores * CAP, 2, PAGE, HD)
    return pl.pallas_call(
        functools.partial(attend_kernel, heads),
        out_shape=jax.ShapeDtypeStruct((block_rows, width), queries.dtype),
        in_specs=[smem, smem, smem, smem, vmem, any_spec, any_spec],
        out_specs=vmem,
        scratch_shapes=[
            pltpu.VMEM((requests, 2, keys, HD), jnp.bfloat16),
            pltpu.VMEM((2, block_rows, HD), jnp.bfloat16),
            pltpu.VMEM(((keys + 2 * KEYS + KEYS) // KEYS, stack, KEYS), jnp.float32),
            pltpu.VMEM((stack, HD), jnp.float32),
            pltpu.VMEM((stack, 2 * HD), jnp.float32),
            pltpu.SMEM((stores,), jnp.int32),
            pltpu.SemaphoreType.DMA((requests, pages, 2)),
            pltpu.SemaphoreType.DMA,
        ],
        compiler_params=pltpu.CompilerParams(vmem_limit_bytes=40 << 20),
        name="attend",
    )(page_host, page_slot, prefix_len, fresh_len, queries, new_kv, flat)


def local(queries, fresh_kv, page_pool, page_host, page_slot, prefix_len, fresh_len):
    stores = lax.axis_size("store")
    tps = lax.axis_size("tp")
    requests, pages = page_host.shape
    entries = requests * pages
    page = lax.broadcasted_iota(jnp.int32, (requests, pages), 1)
    entry = lax.broadcasted_iota(jnp.int32, (requests, pages), 0) * pages + page
    in_use = page * PAGE < prefix_len[:, None]
    codes = jnp.where(in_use, page_host, stores) * 4096 + entry * 64 + page_slot
    codes = codes.reshape(1, entries)
    codes = jnp.pad(codes, ((0, 0), (0, LANES - entries)), constant_values=stores * 4096)
    codes = jnp.broadcast_to(codes, (8, LANES))
    arrived, new_kv = exchange(codes, fresh_kv, page_pool, stores, tps)
    return attention(queries, new_kv, arrived, page_host, page_slot, prefix_len, fresh_len)


def solution(mesh):
    placed = (
        P("store", "tp"),
        P(None, ("store", "tp"), None),
        P("store", None, None, "tp"),
        P("store", None),
        P("store", None),
        P("store"),
        P("store", None),
    )
    return jax.shard_map(
        local, mesh=mesh, in_specs=placed, out_specs=P("store", "tp"), check_vma=False
    )
```

time: 315 us -> 175 us (0.56)
  the two profiles are of different devices: /device:TPU:40 before, /device:TPU:170 now
where the time goes in v1:
time: 175 us
  Pallas kernels  171 us (98%)
  local copies, waits for them, and re-layouts  3.35 us (2%)
    pallas_call x1, Pallas kernels, exchange(): pl.pallas_call(functools.partial(exchange_kernel, stores, tps), out_shape...  109 us
    pallas_call x1, Pallas kernels, attention(): pl.pallas_call(functools.partial(attend_kernel, heads), out_shape=jax.Sha...  61.7 us

profile of v1, /device:TPU:170, one launch (start us, length us, event | category | flops | bytes accessed | tf_op | source)
XLA Modules:
  0.0 175.2 jit_solution(940308502839083671)
XLA Ops:
  0.0 0.0 copy-start.5
  0.0 0.0 copy-start.4
  0.0 0.0 copy-start.3
  0.0 0.0 copy-start.6
  0.0 0.8 add_add_fusion
  0.8 0.1 reshape.7
  0.9 0.0 copy-start
  0.9 2.2 %copy-done = bf16[64,2,128,128]{3,2,1,0:T(8,128)(2,1)S(1)} copy-done((bf16[64,2,128,128]{3,2,1,0:T(8,128)(2,1)S(1)}, bf16[64,2,128,128]{3,2,1,0:T(8,128)(2,1)}, u32[]{:S(2)}) %copy-start) | copy-done | bytes 4194328
  3.1 0.0 copy-start.2
  3.1 1.0 copy-done.2
  4.2 0.0 copy-start.1
  4.2 109.2 %exchange.1 = (bf16[32,2,2,128,128]{4,3,2,1,0:T(8,128)(2,1)S(1)}, bf16[2,1024,128]{2,1,0:T(8,128)(2,1)S(1)}) custom-call(s32[8,128]{1,0:T(8,128)S(1)} %broadcast_in_dim.14.codes_ref, bf16[2,128,1024]{2,1,0:T(8,128)(2,1)S(1)} %copy-done.2, bf16[64,2,128,128]{3,2,1,0:T(8,128)(2,1)S(1)} %copy-done), custom_call_target="tpu_custom_call" | custom-call | tf_op jit(solution)/shard_map/exchange/pallas_call | solution.py:141
  113.4 0.0 copy-done.5
  113.4 0.0 copy-done.4
  113.4 0.0 copy-done.3
  113.5 0.0 copy-done.6
  113.5 0.0 copy-done.1
  113.5 61.7 %attend.1 = bf16[1024,1024]{1,0:T(8,128)(2,1)} custom-call(s32[4,8]{1,0:T(4,128)S(1)} %copy-done.3, s32[4,8]{1,0:T(4,128)S(1)} %copy-done.4, s32[4]{0:T(128)S(1)} %copy-done.5, s32[1,4]{1,0:T(1,128)S(1)} %copy-done.6, bf16[1024,1024]{1,0:T(8,128)(2,1)S(1)} %copy-done.1, bf16[2,1024,128]{2,1,0:T(8,128)(2,1)S(1)} %get-tuple-element.7.new_ref, ...), custom_call_target="tpu_custom_call" | custom-call | tf_op jit(solution)/shard_map/attend/pallas_call | solution.py:314
  (4 shorter events, 0.0 us)
Async XLA Ops:
  0.0 113.4 %copy-start.5 = (s32[4]{0:T(128)S(1)}, s32[4]{0:T(128)}, u32[]{:S(2)}) copy-start(s32[4]{0:T(128)} %prefix_s.1) | copy-start | bytes 52
  0.0 113.4 %copy-start.4 = (s32[4,8]{1,0:T(4,128)S(1)}, s32[4,8]{1,0:T(4,128)}, u32[]{:S(2)}) copy-start(s32[4,8]{1,0:T(4,128)} %slot_s.1) | copy-start | bytes 388
  0.0 113.4 %copy-start.3 = (s32[4,8]{1,0:T(4,128)S(1)}, s32[4,8]{1,0:T(4,128)}, u32[]{:S(2)}) copy-start(s32[4,8]{1,0:T(4,128)} %host_s.1) | copy-start | bytes 388
  0.0 113.4 %copy-start.6 = (s32[1,4]{1,0:T(1,128)S(1)}, s32[1,4]{1,0:T(1,128)}, u32[]{:S(2)}) copy-start(s32[1,4]{1,0:T(1,128)} %length_s.1) | copy-start | bytes 52
  0.9 2.2 %copy-start = (bf16[64,2,128,128]{3,2,1,0:T(8,128)(2,1)S(1)}, bf16[64,2,128,128]{3,2,1,0:T(8,128)(2,1)}, u32[]{:S(2)}) copy-start(bf16[64,2,128,128]{3,2,1,0:T(8,128)(2,1)} %pool_ref.1) | copy-start | bytes 12582916
  3.1 1.0 copy-start.2
  4.2 109.3 %copy-start.1 = (bf16[1024,1024]{1,0:T(8,128)(2,1)S(1)}, bf16[1024,1024]{1,0:T(8,128)(2,1)}, u32[]{:S(2)}) copy-start(bf16[1024,1024]{1,0:T(8,128)(2,1)} %q_ref.1) | copy-start | bytes 6291460

commit v2 on v1

v2 whole, which is shorter than its diff:
```python
import functools
import math

import jax
import jax.numpy as jnp
from jax import lax
from jax.experimental import pallas as pl
from jax.experimental.pallas import tpu as pltpu
from jax.sharding import PartitionSpec as P

HD = 128
PAGE = 128
CAP = 2
NEG = -1e30
MESH = pl.DeviceIdType.MESH
LANES = 128


def exchange_kernel(
    stores, tps, codes_ref, fresh_ref, pool_ref, arrived_ref, new_ref,
    want, got, got_s, pool_v, send_v,
    local_sem, want_send, want_recv, page_send, page_recv, new_send, new_recv,
):
    me = lax.axis_index("store")
    mt = lax.axis_index("tp")
    slots = pool_v.shape[0]

    pool_copy = pltpu.make_async_copy(pool_ref, pool_v, local_sem.at[0])
    pool_copy.start()
    own_new = pltpu.make_async_copy(
        fresh_ref.at[:, :, pl.ds(pl.multiple_of(mt * HD, HD), HD)],
        new_ref.at[mt],
        local_sem.at[1],
    )
    own_new.start()

    barrier = pltpu.get_barrier_semaphore()

    def greet_store(i, c):
        d = lax.rem(me + i, stores)
        pl.semaphore_signal(barrier, inc=1, device_id={"store": d}, device_id_type=MESH)
        return c

    def greet_tp(i, c):
        d = lax.rem(mt + i, tps)
        pl.semaphore_signal(barrier, inc=1, device_id={"tp": d}, device_id_type=MESH)
        return c

    lax.fori_loop(1, stores, greet_store, 0)
    lax.fori_loop(1, tps, greet_tp, 0)

    codes = codes_ref[0:1, :]
    owner = lax.shift_right_arithmetic(codes, 12)
    item = jnp.bitwise_and(codes, 4095)
    source = lax.broadcasted_iota(jnp.int32, (stores, LANES), 0)
    lane = lax.broadcasted_iota(jnp.int32, (stores, LANES), 1)
    match = jnp.broadcast_to(owner, (stores, LANES)) == source
    item = jnp.broadcast_to(item, (stores, LANES))
    first = jnp.min(jnp.where(match, item, 4095), axis=1, keepdims=True)
    second = jnp.max(jnp.where(match, item, 0), axis=1, keepdims=True)
    both = jnp.where(lane == 0, first, second)
    want[...] = jnp.bitwise_and(both, slots - 1).reshape(stores, 1, LANES)

    pl.semaphore_wait(barrier, stores - 1 + tps - 1)

    def new_copy(i):
        d = lax.rem(mt + i, tps)
        return pltpu.make_async_remote_copy(
            src_ref=fresh_ref.at[:, :, pl.ds(pl.multiple_of(d * HD, HD), HD)],
            dst_ref=new_ref.at[mt],
            send_sem=new_send.at[i],
            recv_sem=new_recv.at[i],
            device_id={"tp": d},
            device_id_type=MESH,
        )

    def want_copy(i):
        d = lax.rem(me + i, stores)
        return pltpu.make_async_remote_copy(
            src_ref=want.at[d],
            dst_ref=got.at[me],
            send_sem=want_send.at[i],
            recv_sem=want_recv.at[i],
            device_id={"store": d},
            device_id_type=MESH,
        )

    def page_copy(i):
        d = lax.rem(me + i, stores)
        return pltpu.make_async_remote_copy(
            src_ref=send_v.at[d],
            dst_ref=arrived_ref.at[me],
            send_sem=page_send.at[i],
            recv_sem=page_recv.at[i],
            device_id={"store": d},
            device_id_type=MESH,
        )

    def run(start, stop, body):
        def step(i, c):
            body(i)
            return c
        lax.fori_loop(start, stop, step, 0)

    run(1, stores, lambda i: want_copy(i).start())
    run(1, tps, lambda i: new_copy(i).start())
    got_own = pltpu.make_async_copy(want.at[me], got.at[me], local_sem.at[2])
    got_own.start()
    got_own.wait()
    run(1, stores, lambda i: want_copy(i).wait())
    scalars = pltpu.make_async_copy(got, got_s, local_sem.at[3])
    scalars.start()
    pool_copy.wait()
    scalars.wait()

    def pack(i):
        d = lax.rem(me + i, stores)
        send_v[d, 0] = pool_v[got_s[d, 0, 0]]
        send_v[d, 1] = pool_v[got_s[d, 0, 1]]

    def pack_send(i):
        pack(i)
        page_copy(i).start()

    run(1, stores, pack_send)
    pack(0)
    own = pltpu.make_async_copy(send_v.at[me], arrived_ref.at[me], local_sem.at[4])
    own.start()
    own.wait()
    own_new.wait()
    run(1, tps, lambda i: new_copy(i).wait())
    run(1, stores, lambda i: page_copy(i).wait())


def exchange(codes, fresh_kv, page_pool, stores, tps):
    slots, _, page, width = page_pool.shape
    rows = fresh_kv.shape[1]
    dt = page_pool.dtype
    any_spec = pl.BlockSpec(memory_space=pl.ANY)
    hbm_spec = pl.BlockSpec(memory_space=pltpu.HBM)
    return pl.pallas_call(
        functools.partial(exchange_kernel, stores, tps),
        out_shape=(
            jax.ShapeDtypeStruct((stores, CAP, 2, page, width), dt),
            jax.ShapeDtypeStruct((tps, 2, rows, HD), dt),
        ),
        in_specs=[pl.BlockSpec(memory_space=pltpu.VMEM), hbm_spec, hbm_spec],
        out_specs=(any_spec, any_spec),
        scratch_shapes=[
            pltpu.VMEM((stores, 1, LANES), jnp.int32),
            pltpu.VMEM((stores, 1, LANES), jnp.int32),
            pltpu.SMEM((stores, 1, LANES), jnp.int32),
            pltpu.VMEM((slots, 2, page, width), dt),
            pltpu.VMEM((stores, CAP, 2, page, width), dt),
            pltpu.SemaphoreType.DMA((5,)),
            pltpu.SemaphoreType.DMA((stores,)),
            pltpu.SemaphoreType.DMA((stores,)),
            pltpu.SemaphoreType.DMA((stores,)),
            pltpu.SemaphoreType.DMA((stores,)),
            pltpu.SemaphoreType.DMA((tps,)),
            pltpu.SemaphoreType.DMA((tps,)),
        ],
        compiler_params=pltpu.CompilerParams(
            collective_id=0, has_side_effects=True, vmem_limit_bytes=24 << 20
        ),
        name="exchange",
    )(codes, fresh_kv, page_pool)


ROWS = 64
KEYS = 256
FAR = 1 << 20


def attend_kernel(
    heads, host_s, prefix_s, length_s, q_ref, new_ref, arrived_ref, out_ref,
    kv, row_id, scores, count, page_sem, new_sem,
):
    requests, pages = host_s.shape
    stores = count.shape[0]
    blocks = new_ref.shape[0]
    cached_pages = requests * pages
    scale = math.log2(math.e) / math.sqrt(HD)
    stack = ROWS * heads

    new_copy = pltpu.make_async_copy(new_ref, kv.at[pl.ds(cached_pages, blocks)], new_sem)
    new_copy.start()

    def clear(i, c):
        count[i] = 0
        return c

    lax.fori_loop(0, stores, clear, 0)

    def page_copy(r, p, at):
        return pltpu.make_async_copy(
            arrived_ref.at[at], kv.at[r * pages + p], page_sem.at[r, p]
        )

    def used_pages(r):
        return lax.div(prefix_s[r] + (PAGE - 1), PAGE)

    for r in range(requests):
        def fetch(p, c):
            host = host_s[r, p]
            rank = count[host]
            count[host] = rank + 1
            page_copy(r, p, host * CAP + jnp.minimum(rank, CAP - 1)).start()
            return c

        lax.fori_loop(0, used_pages(r), fetch, 0)

    row_id[...] = (
        lax.broadcasted_iota(jnp.int32, (stack, HD), 1)
        == lax.rem(lax.broadcasted_iota(jnp.int32, (stack, HD), 0), ROWS)
    ).astype(jnp.bfloat16)
    key_row = lax.broadcasted_iota(jnp.int32, (PAGE, HD), 0)
    key_lane = lax.broadcasted_iota(jnp.int32, (PAGE, HD), 1)
    ones = jnp.ones((PAGE, HD), jnp.bfloat16)
    no_mask = jnp.zeros((PAGE, HD), jnp.bfloat16)
    out_row = lax.broadcasted_iota(jnp.int32, (ROWS, HD), 0)
    new_copy.wait()

    def one_request(r, offset):
        length = length_s[0, r]
        prefix = prefix_s[r]
        used = used_pages(r)
        full = lax.div(prefix, PAGE)

        def wait_page(p, c):
            page_copy(r, p, 0).wait()
            return c

        lax.fori_loop(0, used, wait_page, 0)

        def one_block(b, c):
            row0 = pl.multiple_of(b * ROWS, ROWS)
            f0 = lax.div(offset, PAGE)
            f1 = lax.div(row0 + (ROWS - 1), PAGE) + 1
            total = used + f1 - f0

            def place(i):
                cached = i < used
                return jnp.where(
                    cached, r * pages + i, cached_pages + jnp.minimum(f0 + i - used, f1 - 1)
                )

            def mask(i):
                if i < 4:
                    return no_mask
                cached = i < used
                base = PAGE * (f0 + i - used)
                low = jnp.where(cached, 0, jnp.where(i < total, offset - base, FAR))
                high = jnp.where(cached, prefix - 1 - PAGE * i, row0 - base)
                slope = jnp.where(cached, 0, 1)
                ok = (key_row >= low) & (key_row <= high + key_lane * slope)
                return jnp.where(ok, 0.0, NEG).astype(jnp.bfloat16)

            q = q_ref[pl.ds(row0, ROWS), :]
            q = jnp.concatenate([q[:, h * HD:(h + 1) * HD] for h in range(heads)], axis=0)
            q = jnp.concatenate([q, row_id[...]], axis=1)
            mine = (out_row + row0 >= offset) & (out_row + row0 < offset + length)

            def variant(chunks):
                def body():
                    for j in range(chunks):
                        k = jnp.concatenate(
                            [
                                jnp.concatenate([kv[place(i), 0], mask(i)], axis=1)
                                for i in (2 * j, 2 * j + 1)
                            ],
                            axis=0,
                        )
                        scores[j] = lax.dot_general(
                            q, k, (((1,), (1,)), ((), ())), preferred_element_type=jnp.float32
                        )
                    top = scores[0]
                    for j in range(1, chunks):
                        top = jnp.maximum(top, scores[j])
                    top = jnp.max(top, axis=1, keepdims=True) * scale
                    mixed = None
                    for j in range(chunks):
                        w = jnp.exp2(scores[j] * scale - top).astype(jnp.bfloat16)
                        v = jnp.concatenate(
                            [
                                jnp.concatenate([kv[place(i), 1], ones], axis=1)
                                for i in (2 * j, 2 * j + 1)
                            ],
                            axis=0,
                        )
                        part = jnp.dot(w, v, preferred_element_type=jnp.float32)
                        mixed = part if mixed is None else mixed + part
                    result = (mixed[:, :HD] / mixed[:, HD:]).astype(jnp.bfloat16)
                    for h in range(heads):
                        at = (pl.ds(row0, ROWS), slice(h * HD, (h + 1) * HD))
                        out_ref[at] = jnp.where(
                            mine, result[h * ROWS:(h + 1) * ROWS], out_ref[at]
                        )
                return body

            chunks = lax.div(total + 1, 2)
            for n in range(3, 7):
                pl.when(chunks == n)(variant(n))
            return c

        lax.fori_loop(lax.div(offset, ROWS), lax.div(offset + length - 1, ROWS) + 1, one_block, 0)
        return offset + length

    lax.fori_loop(0, requests, one_request, 0)


def attention(queries, new_kv, arrived, page_host, prefix_len, fresh_len):
    block_rows, width = queries.shape
    requests, pages = page_host.shape
    heads = width // HD
    stores = arrived.shape[0]
    stack = ROWS * heads
    smem = pl.BlockSpec(memory_space=pltpu.SMEM)
    any_spec = pl.BlockSpec(memory_space=pl.ANY)
    vmem = pl.BlockSpec(memory_space=pltpu.VMEM)
    flat = arrived.reshape(stores * CAP, 2, PAGE, HD)
    return pl.pallas_call(
        functools.partial(attend_kernel, heads),
        out_shape=jax.ShapeDtypeStruct((block_rows, width), queries.dtype),
        in_specs=[smem, smem, smem, vmem, any_spec, any_spec],
        out_specs=vmem,
        scratch_shapes=[
            pltpu.VMEM((requests * pages + new_kv.shape[0], 2, PAGE, HD), jnp.bfloat16),
            pltpu.VMEM((stack, HD), jnp.bfloat16),
            pltpu.VMEM((6, stack, KEYS), jnp.float32),
            pltpu.SMEM((stores,), jnp.int32),
            pltpu.SemaphoreType.DMA((requests, pages)),
            pltpu.SemaphoreType.DMA,
        ],
        compiler_params=pltpu.CompilerParams(vmem_limit_bytes=40 << 20),
        name="attend",
    )(page_host, prefix_len, fresh_len, queries, new_kv, flat)


def local(queries, fresh_kv, page_pool, page_host, page_slot, prefix_len, fresh_len):
    stores = lax.axis_size("store")
    tps = lax.axis_size("tp")
    requests, pages = page_host.shape
    entries = requests * pages
    page = lax.broadcasted_iota(jnp.int32, (requests, pages), 1)
    entry = lax.broadcasted_iota(jnp.int32, (requests, pages), 0) * pages + page
    in_use = page * PAGE < prefix_len[:, None]
    codes = jnp.where(in_use, page_host, stores) * 4096 + entry * 64 + page_slot
    codes = codes.reshape(1, entries)
    codes = jnp.pad(codes, ((0, 0), (0, LANES - entries)), constant_values=stores * 4096)
    codes = jnp.broadcast_to(codes, (8, LANES))
    arrived, new_kv = exchange(codes, fresh_kv, page_pool, stores, tps)
    return attention(queries, new_kv, arrived, page_host, prefix_len, fresh_len)


def solution(mesh):
    placed = (
        P("store", "tp"),
        P(None, ("store", "tp"), None),
        P("store", None, None, "tp"),
        P("store", None),
        P("store", None),
        P("store"),
        P("store", None),
    )
    return jax.shard_map(
        local, mesh=mesh, in_specs=placed, out_specs=P("store", "tp"), check_vma=False
    )
```

time: 175 us -> 151 us (0.86)
  the two profiles are of different devices: /device:TPU:170 before, /device:TPU:24 now
where the time goes in v2:
time: 151 us
  Pallas kernels  147 us (97%)
  local copies, waits for them, and re-layouts  3.34 us (2%)
    pallas_call x1, Pallas kernels, exchange(): pl.pallas_call(functools.partial(exchange_kernel, stores, tps), out_shape...  110 us
    pallas_call x1, Pallas kernels, attention(): pl.pallas_call(functools.partial(attend_kernel, heads), out_shape=jax.Sha...  37.3 us
    unnamed x12, local copies, waits for them, and re-layouts  3.24 us

profile of v2, /device:TPU:24, one launch (start us, length us, event | category | flops | bytes accessed | tf_op | source)
XLA Modules:
  0.0 151.3 jit_solution(12864205915218660899)
XLA Ops:
  0.0 0.0 copy-start.4
  0.0 0.0 copy-start.3
  0.0 0.0 copy-start.5
  0.0 0.8 add_add_fusion
  0.8 0.1 reshape.7
  0.9 0.0 copy-start
  0.9 2.2 %copy-done = bf16[64,2,128,128]{3,2,1,0:T(8,128)(2,1)S(1)} copy-done((bf16[64,2,128,128]{3,2,1,0:T(8,128)(2,1)S(1)}, bf16[64,2,128,128]{3,2,1,0:T(8,128)(2,1)}, u32[]{:S(2)}) %copy-start) | copy-done | bytes 4194328
  3.1 0.0 copy-start.2
  3.1 1.0 copy-done.2
  4.2 0.0 copy-start.1
  4.2 109.7 %exchange.1 = (bf16[32,2,2,128,128]{4,3,2,1,0:T(8,128)(2,1)S(1)}, bf16[8,2,128,128]{3,2,1,0:T(8,128)(2,1)S(1)}) custom-call(s32[8,128]{1,0:T(8,128)S(1)} %broadcast_in_dim.14.codes_ref, bf16[2,128,1024]{2,1,0:T(8,128)(2,1)S(1)} %copy-done.2, bf16[64,2,128,128]{3,2,1,0:T(8,128)(2,1)S(1)} %copy-done), custom_call_target="tpu_custom_call" | custom-call | tf_op jit(solution)/shard_map/exchange/pallas_call | solution.py:141
  113.9 0.0 copy-done.4
  113.9 0.0 copy-done.3
  113.9 0.0 copy-done.5
  113.9 0.0 copy-done.1
  113.9 37.3 %attend.1 = bf16[1024,1024]{1,0:T(8,128)(2,1)} custom-call(s32[4,8]{1,0:T(4,128)S(1)} %copy-done.3, s32[4]{0:T(128)S(1)} %copy-done.4, s32[1,4]{1,0:T(1,128)S(1)} %copy-done.5, bf16[1024,1024]{1,0:T(8,128)(2,1)S(1)} %copy-done.1, bf16[8,2,128,128]{3,2,1,0:T(8,128)(2,1)S(1)} %get-tuple-element.7.new_ref, bf16[64,2,128,128]{3,2,1,0:T(8,128)(2,1)S(1)} %bitcast.3), custom_call_target="tpu_custom_call" | custom-call | tf_op jit(solution)/shard_map/attend/pallas_call | solution.py:322
  (4 shorter events, 0.0 us)
Async XLA Ops:
  0.0 113.9 %copy-start.4 = (s32[4]{0:T(128)S(1)}, s32[4]{0:T(128)}, u32[]{:S(2)}) copy-start(s32[4]{0:T(128)} %prefix_s.1) | copy-start | bytes 52
  0.0 113.9 %copy-start.3 = (s32[4,8]{1,0:T(4,128)S(1)}, s32[4,8]{1,0:T(4,128)}, u32[]{:S(2)}) copy-start(s32[4,8]{1,0:T(4,128)} %host_s.1) | copy-start | bytes 388
  0.0 113.9 %copy-start.5 = (s32[1,4]{1,0:T(1,128)S(1)}, s32[1,4]{1,0:T(1,128)}, u32[]{:S(2)}) copy-start(s32[1,4]{1,0:T(1,128)} %length_s.1) | copy-start | bytes 52
  0.9 2.2 %copy-start = (bf16[64,2,128,128]{3,2,1,0:T(8,128)(2,1)S(1)}, bf16[64,2,128,128]{3,2,1,0:T(8,128)(2,1)}, u32[]{:S(2)}) copy-start(bf16[64,2,128,128]{3,2,1,0:T(8,128)(2,1)} %pool_ref.1) | copy-start | bytes 12582916
  3.1 1.0 copy-start.2
  4.2 109.8 %copy-start.1 = (bf16[1024,1024]{1,0:T(8,128)(2,1)S(1)}, bf16[1024,1024]{1,0:T(8,128)(2,1)}, u32[]{:S(2)}) copy-start(bf16[1024,1024]{1,0:T(8,128)(2,1)} %q_ref.1) | copy-start | bytes 6291460

commit v3 on v0

v3 whole, which is shorter than its diff:
```python
import functools
import math

import jax
import jax.numpy as jnp
from jax import lax
from jax.experimental import pallas as pl
from jax.experimental.pallas import tpu as pltpu
from jax.sharding import PartitionSpec as P

HD = 128
PAGE = 128
LANES = 128
NEG = -1e30
FAR = 1 << 20
MESH = pl.DeviceIdType.MESH
RING = 8
ROWS = 64
EARLY = 10
SCALE = math.log2(math.e) / math.sqrt(HD)


def plan_kernel(host_s, slot_s, prefix_s, want_ref, plan_s, want_s, count, sem):
    requests, pages = host_s.shape
    stores = count.shape[0]
    entries = requests * pages

    def clear(i, c):
        count[i] = 0
        want_s[i, 0, 0] = 0
        want_s[i, 0, 1] = 0
        return c

    lax.fori_loop(0, stores, clear, 0)
    for r in range(requests):
        prefix = prefix_s[r]

        def one(p, c):
            n0, n1 = c
            host = host_s[r, p]
            rank = jnp.minimum(count[host], 1)
            count[host] = rank + 1
            want_s[host, 0, rank] = slot_s[r, p]
            at = rank * entries + r * pages + jnp.where(rank == 0, n0, n1)
            plan_s[at] = host * 256 + jnp.minimum(prefix - p * PAGE, PAGE)
            return n0 + 1 - rank, n1 + rank

        n0, n1 = lax.fori_loop(0, lax.div(prefix + (PAGE - 1), PAGE), one, (0, 0))
        plan_s[2 * entries + r] = n0
        plan_s[2 * entries + requests + r] = n1
    copy = pltpu.make_async_copy(want_s, want_ref, sem)
    copy.start()
    copy.wait()


def make_plan(page_host, page_slot, prefix_len, stores):
    requests, pages = page_host.shape
    smem = pl.BlockSpec(memory_space=pltpu.SMEM)
    return pl.pallas_call(
        plan_kernel,
        out_shape=(
            jax.ShapeDtypeStruct((stores, 1, LANES), jnp.int32),
            jax.ShapeDtypeStruct((2 * requests * pages + 2 * requests,), jnp.int32),
        ),
        in_specs=[smem, smem, smem],
        out_specs=(pl.BlockSpec(memory_space=pl.ANY), smem),
        scratch_shapes=[
            pltpu.SMEM((stores, 1, LANES), jnp.int32),
            pltpu.SMEM((stores,), jnp.int32),
            pltpu.SemaphoreType.DMA,
        ],
        name="plan",
    )(page_host, page_slot, prefix_len)


def one_hot_rows(stack):
    lane = lax.broadcasted_iota(jnp.int32, (stack, HD), 1)
    row = lax.rem(lax.broadcasted_iota(jnp.int32, (stack, HD), 0), ROWS)
    return (lane == row).astype(jnp.bfloat16)


def stacked(q, row_id, heads):
    q = jnp.concatenate([q[:, h * HD:(h + 1) * HD] for h in range(heads)], axis=0)
    return jnp.concatenate([q, row_id], axis=1)


def page_mask(low, high, slope):
    key = lax.broadcasted_iota(jnp.int32, (PAGE, HD), 0)
    lane = lax.broadcasted_iota(jnp.int32, (PAGE, HD), 1)
    ok = (key >= low) & (key <= high + lane * slope)
    return jnp.where(ok, 0.0, NEG).astype(jnp.bfloat16)


def attend_pages(q, keys, values, scores, top):
    chunks = len(keys) // 2
    ones = jnp.ones((PAGE, HD), jnp.bfloat16)
    for j in range(chunks):
        k = jnp.concatenate(
            [jnp.concatenate(keys[i](), axis=1) for i in (2 * j, 2 * j + 1)], axis=0
        )
        scores[j] = lax.dot_general(
            q, k, (((1,), (1,)), ((), ())), preferred_element_type=jnp.float32
        )
    best = scores[0]
    for j in range(1, chunks):
        best = jnp.maximum(best, scores[j])
    best = jnp.max(best, axis=1, keepdims=True) * SCALE
    top = best if top is None else jnp.maximum(top, best)
    mixed = None
    for j in range(chunks):
        w = jnp.exp2(scores[j] * SCALE - top).astype(jnp.bfloat16)
        v = jnp.concatenate(
            [jnp.concatenate([values[i](), ones], axis=1) for i in (2 * j, 2 * j + 1)], axis=0
        )
        part = jnp.dot(w, v, preferred_element_type=jnp.float32)
        mixed = part if mixed is None else mixed + part
    return top, mixed


def exchange_kernel(
    stores, tps, heads, plan_s, length_s, want, fresh_ref, pool_ref, q_ref,
    pages_ref, late_ref, state_ref,
    got, got_s, pool_v, send_v, q_v, row_id, scores, state,
    local_sem, state_sem, q_sem, want_send, want_recv, page_send, page_recv, new_send, new_recv,
):
    me = lax.axis_index("store")
    mt = lax.axis_index("tp")
    my_y, my_z = me // RING, me % RING
    requests = length_s.shape[1]
    items = state_ref.shape[0]
    stack = ROWS * heads
    entries = (plan_s.shape[0] - 2 * requests) // 2
    pages = entries // requests

    def local_copy(src, dst, n):
        return pltpu.make_async_copy(src, dst, local_sem.at[n])

    pool_copy = local_copy(pool_ref, pool_v, 0)
    pool_copy.start()
    own_new = local_copy(
        fresh_ref.at[:, :, pl.ds(pl.multiple_of(mt * HD, HD), HD)], pages_ref.at[stores + mt], 1
    )
    own_new.start()
    blocks = q_v.shape[0]

    def q_copy(i):
        return pltpu.make_async_copy(
            q_ref.at[pl.ds(pl.multiple_of(i * ROWS, ROWS), ROWS), :], q_v.at[i], q_sem.at[i]
        )


    def run(start, stop, body):
        def step(i, c):
            body(i)
            return c
        lax.fori_loop(start, stop, step, 0)

    def partner(i):
        turn = i // (stores // RING)
        half = (turn + 1) // 2
        odd = turn % 2
        dz = odd * half + (1 - odd) * (RING - half)
        dy = i % (stores // RING)
        return ((my_y + dy) % (stores // RING)) * RING + (my_z + dz) % RING

    run(0, blocks, lambda i: q_copy(i).start())
    barrier = pltpu.get_barrier_semaphore()

    def greet(axis, d):
        pl.semaphore_signal(barrier, inc=1, device_id={axis: d}, device_id_type=MESH)

    run(1, stores, lambda i: greet("store", partner(i)))
    run(1, tps, lambda i: greet("tp", (mt + i) % tps))
    pl.semaphore_wait(barrier, stores - 1 + tps - 1)

    def remote(src, dst, send, recv, axis, d):
        return pltpu.make_async_remote_copy(
            src_ref=src, dst_ref=dst, send_sem=send, recv_sem=recv,
            device_id={axis: d}, device_id_type=MESH,
        )

    def new_copy(i):
        d = (mt + i) % tps
        return remote(
            fresh_ref.at[:, :, pl.ds(pl.multiple_of(d * HD, HD), HD)],
            pages_ref.at[stores + mt], new_send.at[i], new_recv.at[i], "tp", d,
        )

    def want_copy(i):
        d = partner(i)
        return remote(want.at[d], got.at[me], want_send.at[i], want_recv.at[i], "store", d)

    def page_copy(k, i):
        d = partner(i)
        dst = pages_ref.at[me] if k == 0 else late_ref.at[me]
        return remote(
            send_v.at[k, d], dst, page_send.at[k, i], page_recv.at[k, i], "store", d
        )

    run(1, stores, lambda i: want_copy(i).start())
    run(1, tps, lambda i: new_copy(i).start())
    got_own = local_copy(want.at[me], got.at[me], 3)
    got_own.start()
    row_id[...] = one_hot_rows(stack)
    got_own.wait()
    run(1, stores, lambda i: want_copy(i).wait())
    scalars = local_copy(got, got_s, 4)
    scalars.start()
    pool_copy.wait()
    scalars.wait()

    for k in range(2):
        def pack(i):
            d = partner(i)
            send_v[k, d] = pool_v[got_s[d, 0, k]]
            page_copy(k, i).start()
        run(1, stores, pack)
        send_v[k, me] = pool_v[got_s[me, 0, k]]
    own = [
        local_copy(send_v.at[0, me], pages_ref.at[me], 5),
        local_copy(send_v.at[1, me], late_ref.at[me], 6),
    ]
    for copy in own:
        copy.start()
    for copy in own:
        copy.wait()
    own_new.wait()
    run(0, blocks, lambda i: q_copy(i).wait())
    run(1, tps, lambda i: new_copy(i).wait())
    run(1, stores, lambda i: page_copy(0, i).wait())

    lane = lax.broadcasted_iota(jnp.int32, (stack, HD), 1)

    def one_item(item, c):
        r, row0, offset = find_item(length_s, item)
        f0 = offset // PAGE
        new = (row0 + (ROWS - 1)) // PAGE + 1 - f0
        early = new + plan_s[2 * entries + r]

        def entry(i):
            is_new = i < new
            j = jnp.clip(i - new, 0, pages - 1)
            code = plan_s[r * pages + j]
            base = PAGE * (f0 + i)
            used = i < early
            place = jnp.where(is_new, stores + f0 + i, jnp.where(used, code // 256, 0))
            place = jnp.clip(place, 0, stores + tps - 1)
            low = jnp.where(is_new, offset - base, jnp.where(used, 0, FAR))
            high = jnp.where(is_new, row0 - base, code % 256 - 1)
            return place, page_mask(low, high, jnp.where(is_new, 1, 0))

        def key(i):
            place, mask = entry(i)
            return [pages_ref[place, 0], mask]

        def value(i):
            place, _ = entry(i)
            return pages_ref[place, 1]

        q = stacked(q_v[jnp.clip(row0 // ROWS, 0, blocks - 1)], row_id[...], heads)
        top, mixed = attend_pages(
            q,
            [functools.partial(key, i) for i in range(EARLY)],
            [functools.partial(value, i) for i in range(EARLY)],
            scores, None,
        )
        slot = item % 2

        @pl.when(item >= 2)
        def _():
            state_copy(item - 2).wait()

        state[slot, :, :HD] = mixed[:, :HD]
        state[slot, :, HD:] = jnp.where(lane < HD // 2, mixed[:, HD:], top)
        state_copy(item).start()
        return c

    def state_copy(item):
        slot = item % 2
        return pltpu.make_async_copy(state.at[slot], state_ref.at[item], state_sem.at[slot])

    lax.fori_loop(0, items, one_item, 0)
    state_copy(items - 2).wait()
    state_copy(items - 1).wait()
    run(1, stores, lambda i: page_copy(1, i).wait())


def find_item(length_s, item):
    requests = length_s.shape[1]
    offset = 0
    start = 0
    r = 0
    row0 = 0
    at = 0
    for q in range(requests):
        length = length_s[0, q]
        first = offset // ROWS
        count = (offset + length - 1) // ROWS - first + 1
        here = item >= start
        block = jnp.maximum(first + jnp.minimum(item - start, count - 1), 0)
        r = jnp.where(here, q, r)
        row0 = jnp.where(here, block * ROWS, row0)
        at = jnp.where(here, offset, at)
        start = start + count
        offset = offset + length
    return r, row0, at


def exchange(plan, want, fresh_len, fresh_kv, page_pool, queries, stores, tps):
    slots, _, page, width = page_pool.shape
    block_rows, columns = queries.shape
    heads = columns // HD
    requests = fresh_len.shape[1]
    dt = page_pool.dtype
    items = block_rows // ROWS + requests - 1
    stack = ROWS * heads
    smem = pl.BlockSpec(memory_space=pltpu.SMEM)
    vmem = pl.BlockSpec(memory_space=pltpu.VMEM)
    any_spec = pl.BlockSpec(memory_space=pl.ANY)
    sem = pltpu.SemaphoreType.DMA
    return pl.pallas_call(
        functools.partial(exchange_kernel, stores, tps, heads),
        out_shape=(
            jax.ShapeDtypeStruct((stores + tps, 2, page, width), dt),
            jax.ShapeDtypeStruct((stores, 2, page, width), dt),
            jax.ShapeDtypeStruct((items, stack, 2 * HD), jnp.float32),
        ),
        in_specs=[smem, smem, any_spec, any_spec, any_spec, any_spec],
        out_specs=(vmem, any_spec, any_spec),
        scratch_shapes=[
            pltpu.VMEM((stores, 1, LANES), jnp.int32),
            pltpu.SMEM((stores, 1, LANES), jnp.int32),
            pltpu.VMEM((slots, 2, page, width), dt),
            pltpu.VMEM((2, stores, 2, page, width), dt),
            pltpu.VMEM((block_rows // ROWS, ROWS, columns), dt),
            pltpu.VMEM((stack, HD), jnp.bfloat16),
            pltpu.VMEM((EARLY // 2, stack, 2 * PAGE), jnp.float32),
            pltpu.VMEM((2, stack, 2 * HD), jnp.float32),
            sem((7,)),
            sem((2,)),
            sem((block_rows // ROWS,)),
            sem((stores,)),
            sem((stores,)),
            sem((2, stores)),
            sem((2, stores)),
            sem((tps,)),
            sem((tps,)),
        ],
        compiler_params=pltpu.CompilerParams(
            collective_id=0, has_side_effects=True, vmem_limit_bytes=36 << 20
        ),
        name="exchange",
    )(plan, fresh_len, want, fresh_kv, page_pool, queries)


def finish_kernel(
    heads, plan_s, length_s, q_ref, state_ref, pages_ref, late_ref, out_ref,
    late, row_id, scores, state, sem, state_sem,
):
    requests = length_s.shape[1]
    stack = ROWS * heads
    stores = late.shape[0]
    entries = (plan_s.shape[0] - 2 * requests) // 2
    pages = entries // requests
    copy = pltpu.make_async_copy(late_ref, late, sem)
    copy.start()
    items = state_ref.shape[0]

    def state_copy(item):
        slot = item % 2
        return pltpu.make_async_copy(state_ref.at[item], state.at[slot], state_sem.at[slot])

    state_copy(0).start()
    row_id[...] = one_hot_rows(stack)
    out_row = lax.broadcasted_iota(jnp.int32, (ROWS, HD), 0)
    copy.wait()

    def one_request(r, carry):
        offset, item0 = carry
        length = length_s[0, r]
        n0 = plan_s[2 * entries + r]
        n1 = plan_s[2 * entries + requests + r]
        b0 = offset // ROWS
        b1 = (offset + length - 1) // ROWS + 1

        def one_block(b, c):
            row0 = pl.multiple_of(b * ROWS, ROWS)
            item = item0 + b - b0
            slot = item % 2
            state_copy(item).wait()

            @pl.when(item + 1 < items)
            def _():
                state_copy(item + 1).start()

            f0 = offset // PAGE
            new = (row0 + (ROWS - 1)) // PAGE + 1 - f0
            done = jnp.minimum(new + n0, EARLY) - new
            left = n0 - done + n1
            mine = (out_row + row0 >= offset) & (out_row + row0 < offset + length)

            def entry(i):
                j = done + i
                late_one = j >= n0
                code = jnp.where(
                    late_one,
                    plan_s[entries + r * pages + jnp.minimum(j - n0, pages - 1) * jnp.where(late_one, 1, 0)],
                    plan_s[r * pages + jnp.minimum(j, pages - 1)],
                )
                used = i < left
                return late_one, jnp.where(used, code // 256, 0), jnp.where(used, code % 256, 0)

            def page(i, half):
                late_one, place, valid = entry(i)
                return jnp.where(late_one, late[place, half], pages_ref[place, half]), valid

            def key(i):
                k, valid = page(i, 0)
                return [k, page_mask(0, valid - 1, 0)]

            def value(i):
                return page(i, 1)[0]

            def variant(chunks):
                def body():
                    acc = state[slot, :, :HD]
                    sums = state[slot, :, HD:]
                    total = jnp.broadcast_to(sums[:, :1], (stack, HD))
                    if chunks:
                        old = sums[:, HD // 2:HD // 2 + 1]
                        q = stacked(q_ref[pl.ds(row0, ROWS), :], row_id[...], heads)
                        top, mixed = attend_pages(
                            q,
                            [functools.partial(key, i) for i in range(2 * chunks)],
                            [functools.partial(value, i) for i in range(2 * chunks)],
                            scores, old,
                        )
                        fade = jnp.broadcast_to(jnp.exp2(old - top), (stack, HD))
                        acc = acc * fade + mixed[:, :HD]
                        total = total * fade + mixed[:, HD:]
                    result = (acc / total).astype(jnp.bfloat16)
                    for h in range(heads):
                        at = (pl.ds(row0, ROWS), slice(h * HD, (h + 1) * HD))
                        out_ref[at] = jnp.where(
                            mine, result[h * ROWS:(h + 1) * ROWS], out_ref[at]
                        )
                return body

            chunks = (left + 1) // 2
            for n in range(pages // 2 + 1):
                pl.when(chunks == n)(variant(n))
            return c

        lax.fori_loop(b0, b1, one_block, 0)
        return offset + length, item0 + b1 - b0

    _, used_items = lax.fori_loop(0, requests, one_request, (0, 0))

    @pl.when(used_items < items)
    def _():
        state_copy(used_items).wait()


def finish(plan, fresh_len, queries, state, pages, late):
    block_rows, columns = queries.shape
    heads = columns // HD
    stack = ROWS * heads
    smem = pl.BlockSpec(memory_space=pltpu.SMEM)
    vmem = pl.BlockSpec(memory_space=pltpu.VMEM)
    return pl.pallas_call(
        functools.partial(finish_kernel, heads),
        out_shape=jax.ShapeDtypeStruct((block_rows, columns), queries.dtype),
        in_specs=[smem, smem, vmem, pl.BlockSpec(memory_space=pl.ANY), vmem, pl.BlockSpec(memory_space=pl.ANY)],
        out_specs=vmem,
        scratch_shapes=[
            pltpu.VMEM(late.shape, late.dtype),
            pltpu.VMEM((stack, HD), jnp.bfloat16),
            pltpu.VMEM((4, stack, 2 * PAGE), jnp.float32),
            pltpu.VMEM((2, stack, 2 * HD), jnp.float32),
            pltpu.SemaphoreType.DMA,
            pltpu.SemaphoreType.DMA((2,)),
        ],
        compiler_params=pltpu.CompilerParams(vmem_limit_bytes=30 << 20),
        name="finish",
    )(plan, fresh_len, queries, state, pages, late)


def in_hbm(x):
    return pltpu.with_memory_space_constraint(x, pltpu.HBM)


def local(queries, fresh_kv, page_pool, page_host, page_slot, prefix_len, fresh_len):
    stores = lax.axis_size("store")
    tps = lax.axis_size("tp")
    want, plan = make_plan(page_host, page_slot, prefix_len, stores)
    pages, late, state = exchange(
        plan, want, fresh_len, in_hbm(fresh_kv), in_hbm(page_pool), in_hbm(queries), stores, tps
    )
    return finish(plan, fresh_len, queries, state, pages, late)


def solution(mesh):
    placed = (
        P("store", "tp"),
        P(None, ("store", "tp"), None),
        P("store", None, None, "tp"),
        P("store", None),
        P("store", None),
        P("store"),
        P("store", None),
    )
    return jax.shard_map(
        local, mesh=mesh, in_specs=placed, out_specs=P("store", "tp"), check_vma=False
    )
```

time: 315 us -> 141 us (0.45); the launches traced: 310 us -> 141 us
  Pallas kernels: 0 us -> 139 us
  matrix products: 77.5 us -> 0 us
  waiting for transfers between devices: 62.1 us -> 0 us
  local copies, waits for them, and re-layouts: 62.7 us -> 1.97 us
  other arithmetic: 60 us -> 0 us
  between operations: 21.5 us -> 0.04 us
  blocking collectives: 18.8 us -> 0 us
  starting transfers between devices: 6.96 us -> 0 us
    pallas_call x0 -> x3, Pallas kernels: none -> 139 us  [the longest x1 113 us: exchange(): pl.pallas_call(functools.partial(exchange_kernel, stores, tps, heads), ou...]
    dot_general x8 -> x0, matrix products: 77.5 us -> none  [the longest x4 40.9 us: attend(): jnp.einsum('kgmn,nkd->mkgd', rounded, value_rows, preferred_element_type=...]
    all_to_all x1 -> x0, waiting for transfers between devices: 50.2 us -> none  [local(): lax.all_to_all(jnp.take(page_pool, lax.all_to_all(buffer, 'store', split_...]
    reduce_sum x6 -> x0, other arithmetic: 38.4 us -> none  [the longest x4 38.1 us: attend(): row_total = jnp.sum(weights, axis=-1)]
    dynamic_update_slice x4 -> x0, local copies, waits for them, and re-layouts: 21.4 us -> none  [local(): lax.dynamic_update_slice_in_dim(output, jnp.where(row_ok[:, None], mixed_...]
    all_to_all x1 -> x0, blocking collectives: 18.8 us -> none  [local(): lax.all_to_all(buffer, 'store', split_axis=0, concat_axis=0, tiled=True)]
    select_n x10 -> x0, other arithmetic: 14.4 us -> none  [the longest x4 7.18 us: local(): jnp.where(row_ok[:, None], mixed_rows, old_rows)]
    all_gather x1 -> x0, waiting for transfers between devices: 11.4 us -> none  [local(): gathered = lax.all_gather(fresh_kv, 'tp', axis=1, tiled=True)]
  transfers between devices with their start and end apart: 2 -> 0, of which waited for: 2 -> 0; matrix products, arithmetic and copies ran while one was open for 8% -> 0% of each run, Pallas kernels for 0% -> 0%
where the time goes in v3:
time: 141 us
  Pallas kernels  139 us (99%)
  local copies, waits for them, and re-layouts  1.97 us (1%)
    pallas_call x1, Pallas kernels, exchange(): pl.pallas_call(functools.partial(exchange_kernel, stores, tps, heads), ou...  113 us
    pallas_call x1, Pallas kernels, finish(): pl.pallas_call(functools.partial(finish_kernel, heads), out_shape=jax.Sha...  23.5 us

profile of v3, /device:TPU:40, one launch (start us, length us, event | category | flops | bytes accessed | tf_op | source)
XLA Modules:
  0.0 140.9 jit_solution(3015877953154413649)
XLA Ops:
  0.0 2.8 %plan.1 = (s32[32,1,128]{2,1,0:T(1,128)}, s32[72]{0:T(128)}) custom-call(s32[4,8]{1,0:T(4,128)} %host_s.1, s32[4,8]{1,0:T(4,128)} %slot_s.1, s32[4]{0:T(128)} %prefix_s.1), custom_call_target="tpu_custom_call" | custom-call | tf_op jit(solution)/shard_map/plan/pallas_call | solution.py:59
  2.8 0.0 copy-start.1
  2.8 0.7 copy-done.1
  3.5 0.0 copy-start.2
  3.5 0.7 copy-done.2
  4.2 0.0 copy-start.3
  4.2 0.6 copy-done.3
  4.8 0.0 copy-start
  4.8 112.5 %exchange.1 = (bf16[40,2,128,128]{3,2,1,0:T(8,128)(2,1)S(1)}, bf16[32,2,128,128]{3,2,1,0:T(8,128)(2,1)S(1)}, f32[19,512,256]{2,1,0:T(8,128)S(1)}) custom-call(s32[72]{0:T(128)S(1)} %copy-done.3, s32[1,4]{1,0:T(1,128)S(1)} %copy-done.2, s32[32,1,128]{2,1,0:T(1,128)S(1)} %copy-done.1, bf16[2,128,1024]{2,1,0:T(8,128)(2,1)} %fresh_ref.1, ...), custom_call_target="tpu_custom_call" | custom-call | tf_op jit(solution)/shard_map/exchange/pallas_call | solution.py:321
  117.3 0.0 copy-done
  117.3 23.5 %finish.1 = bf16[1024,1024]{1,0:T(8,128)(2,1)} custom-call(s32[72]{0:T(128)S(1)} %copy-done.3, s32[1,4]{1,0:T(1,128)S(1)} %copy-done.2, bf16[1024,1024]{1,0:T(8,128)(2,1)S(1)} %copy-done, f32[19,512,256]{2,1,0:T(8,128)S(1)} %get-tuple-element.12.state_ref, bf16[40,2,128,128]{3,2,1,0:T(8,128)(2,1)S(1)} %get-tuple-element.13.pages_ref, ...), custom_call_target="tpu_custom_call" | custom-call | tf_op jit(solution)/shard_map/finish/pallas_call | solution.py:470
Async XLA Ops:
  2.8 0.7 copy-start.1
  3.5 0.7 copy-start.2
  4.2 0.6 copy-start.3
  4.8 112.5 %copy-start = (bf16[1024,1024]{1,0:T(8,128)(2,1)S(1)}, bf16[1024,1024]{1,0:T(8,128)(2,1)}, u32[]{:S(2)}) copy-start(bf16[1024,1024]{1,0:T(8,128)(2,1)} %q_ref.3) | copy-start | bytes 6291460

commit v4 on v3

v4 whole, which is shorter than its diff:
```python
import functools
import math

import jax
import jax.numpy as jnp
from jax import lax
from jax.experimental import pallas as pl
from jax.experimental.pallas import tpu as pltpu
from jax.sharding import PartitionSpec as P

HD = 128
PAGE = 128
LANES = 128
PAGES_MAX = 8
NEG = -1e30
FAR = 1 << 20
MESH = pl.DeviceIdType.MESH
RING = 8
ROWS = 64
MIDDLE = 2
MOST_NEW = 384
NEAR = 2
SCALE = math.log2(math.e) / math.sqrt(HD)


def plan_kernel(host_s, slot_s, prefix_s, length_s, want_ref, plan_out, want_s, count, sem):
    requests, pages = host_s.shape
    stores = count.shape[0]
    entries = requests * pages
    my_z = lax.axis_index("store") % RING

    def clear(i, c):
        count[i] = 0
        want_s[i, 0, 0] = 0
        want_s[i, 0, 1] = 0
        return c

    lax.fori_loop(0, stores, clear, 0)

    def put(at, value):
        want_s[stores, 0, at] = value
        plan_out[at] = value

    for r in range(requests):
        prefix = prefix_s[r]

        def one(p, c):
            n0, n1, n2 = c
            host = host_s[r, p]
            rank = jnp.minimum(count[host], 1)
            count[host] = rank + 1
            want_s[host, 0, rank] = slot_s[r, p]
            away = (host + RING - my_z) % RING
            far = jnp.where((away > NEAR) & (away < RING - NEAR), rank, 0)
            group = rank + far
            at = group * entries + r * pages + jnp.where(rank == 0, n0, jnp.where(far == 0, n1, n2))
            put(at, host * 256 + jnp.minimum(prefix - p * PAGE, PAGE))
            return n0 + 1 - rank, n1 + rank - far, n2 + far

        counts = lax.fori_loop(0, lax.div(prefix + (PAGE - 1), PAGE), one, (0, 0, 0))
        for group in range(3):
            put(3 * entries + group * requests + r, counts[group])
        put(3 * entries + 3 * requests + r, length_s[0, r])
    copy = pltpu.make_async_copy(want_s, want_ref, sem)
    copy.start()
    copy.wait()


def make_plan(page_host, page_slot, prefix_len, fresh_len, stores):
    smem = pl.BlockSpec(memory_space=pltpu.SMEM)
    return pl.pallas_call(
        plan_kernel,
        out_shape=(
            jax.ShapeDtypeStruct((stores + 1, 1, LANES), jnp.int32),
            jax.ShapeDtypeStruct((LANES,), jnp.int32),
        ),
        in_specs=[smem, smem, smem, smem],
        out_specs=(pl.BlockSpec(memory_space=pl.ANY), smem),
        scratch_shapes=[
            pltpu.SMEM((stores + 1, 1, LANES), jnp.int32),
            pltpu.SMEM((stores,), jnp.int32),
            pltpu.SemaphoreType.DMA,
        ],
        name="plan",
    )(page_host, page_slot, prefix_len, fresh_len)


class Plan:
    def __init__(self, get, requests, pages):
        self.get, self.requests, self.pages = get, requests, pages
        self.entries = requests * pages

    def size(self, group, r):
        return self.get(3 * self.entries + group * self.requests + r)

    def length(self, r):
        return self.get(3 * self.entries + 3 * self.requests + r)

    def item(self, item):
        offset = start = r = row0 = at = 0
        for q in range(self.requests):
            length = self.length(q)
            first = offset // ROWS
            count = (offset + length - 1) // ROWS - first + 1
            here = item >= start
            block = jnp.maximum(first + jnp.minimum(item - start, count - 1), 0)
            r = jnp.where(here, q, r)
            row0 = jnp.where(here, block * ROWS, row0)
            at = jnp.where(here, offset, at)
            start = start + count
            offset = offset + length
        return r, row0, at

    def page(self, group, r, i):
        used = i < self.size(group, r)
        code = self.get(
            group * self.entries + r * self.pages + jnp.clip(i, 0, self.pages - 1)
        )
        return jnp.where(used, code // 256, 0), jnp.where(used, code % 256, 0)


def one_hot_rows(stack):
    lane = lax.broadcasted_iota(jnp.int32, (stack, HD), 1)
    row = lax.rem(lax.broadcasted_iota(jnp.int32, (stack, HD), 0), ROWS)
    return (lane == row).astype(jnp.bfloat16)


def stacked(q, row_id, heads):
    q = jnp.concatenate([q[:, h * HD:(h + 1) * HD] for h in range(heads)], axis=0)
    return jnp.concatenate([q, row_id], axis=1)


def page_mask(low, high, slope):
    key = lax.broadcasted_iota(jnp.int32, (PAGE, HD), 0)
    lane = lax.broadcasted_iota(jnp.int32, (PAGE, HD), 1)
    ok = (key >= low) & (key <= high + lane * slope)
    return jnp.where(ok, 0.0, NEG).astype(jnp.bfloat16)


def attend_pages(q, keys, values, scores, top):
    chunks = len(keys) // 2
    ones = jnp.ones((PAGE, HD), jnp.bfloat16)
    for j in range(chunks):
        k = jnp.concatenate(
            [jnp.concatenate(keys[i](), axis=1) for i in (2 * j, 2 * j + 1)], axis=0
        )
        scores[j] = lax.dot_general(
            q, k, (((1,), (1,)), ((), ())), preferred_element_type=jnp.float32
        )
    best = scores[0]
    for j in range(1, chunks):
        best = jnp.maximum(best, scores[j])
    best = jnp.max(jnp.maximum(best[:, :PAGE], best[:, PAGE:]), axis=1, keepdims=True) * SCALE
    best = jnp.broadcast_to(best, (q.shape[0], HD))
    top = best if top is None else jnp.maximum(top, best)
    mixed = None
    for j in range(chunks):
        w = jnp.concatenate(
            [
                jnp.exp2(scores[j, :, half * PAGE:(half + 1) * PAGE] * SCALE - top)
                for half in range(2)
            ],
            axis=1,
        ).astype(jnp.bfloat16)
        v = jnp.concatenate(
            [jnp.concatenate([values[i](), ones], axis=1) for i in (2 * j, 2 * j + 1)], axis=0
        )
        part = jnp.dot(w, v, preferred_element_type=jnp.float32)
        mixed = part if mixed is None else mixed + part
    return top, mixed


def merged(old_acc, old_total, old_top, top, mixed):
    fade = jnp.exp2(old_top - top)
    return old_acc * fade + mixed[:, :HD], old_total * fade + mixed[:, HD:]


def exchange_kernel(
    stores, tps, heads, requests, want, fresh_ref, pool_ref, q_ref,
    near_ref, far_ref, state,
    got, got_s, plan_s, new_ref, pages_ref, pool_v, send_v, q_v, row_id, masks, scores,
    local_sem, q_sem, want_send, want_recv, page_send, page_recv, new_send, new_recv,
):
    me = lax.axis_index("store")
    mt = lax.axis_index("tp")
    my_y, my_z = me // RING, me % RING
    columns = stores // RING
    items = state.shape[0]
    stack = ROWS * heads
    blocks = q_v.shape[0]
    plan = Plan(lambda i: plan_s[0, i], requests, PAGES_MAX)

    def local_copy(src, dst, n):
        return pltpu.make_async_copy(src, dst, local_sem.at[n])

    def q_copy(i):
        return pltpu.make_async_copy(
            q_ref.at[pl.ds(pl.multiple_of(i * ROWS, ROWS), ROWS), :], q_v.at[i], q_sem.at[i]
        )

    def run(start, stop, body):
        def step(i, c):
            body(i)
            return c
        lax.fori_loop(start, stop, step, 0)

    def partner(i):
        turn = i // columns
        half = (turn + 1) // 2
        odd = turn % 2
        dz = odd * half + (1 - odd) * (RING - half)
        return ((my_y + i % columns) % columns) * RING + (my_z + dz) % RING

    last_near = (2 * NEAR + 1) * columns
    barrier = pltpu.get_barrier_semaphore()

    def greet(axis, d):
        pl.semaphore_signal(barrier, inc=1, device_id={axis: d}, device_id_type=MESH)

    run(1, stores, lambda i: greet("store", partner(i)))
    run(1, tps, lambda i: greet("tp", (mt + i) % tps))

    pool_copy = local_copy(pool_ref, pool_v, 0)
    pool_copy.start()
    own_new = local_copy(
        fresh_ref.at[:, :, pl.ds(pl.multiple_of(mt * HD, HD), HD)], new_ref.at[mt], 1
    )
    own_new.start()
    plan_copy = local_copy(want.at[stores], plan_s, 2)
    plan_copy.start()
    got_own = local_copy(want.at[me], got.at[me], 3)
    got_own.start()
    run(0, blocks, lambda i: q_copy(i).start())
    pl.semaphore_wait(barrier, stores - 1 + tps - 1)

    def remote(src, dst, send, recv, axis, d):
        return pltpu.make_async_remote_copy(
            src_ref=src, dst_ref=dst, send_sem=send, recv_sem=recv,
            device_id={axis: d}, device_id_type=MESH,
        )

    def new_copy(i):
        d = (mt + i) % tps
        return remote(
            fresh_ref.at[:, :, pl.ds(pl.multiple_of(d * HD, HD), HD)],
            new_ref.at[mt], new_send.at[i], new_recv.at[i], "tp", d,
        )

    def want_copy(i):
        d = partner(i)
        return remote(want.at[d], got.at[me], want_send.at[i], want_recv.at[i], "store", d)

    def page_copy(k, dst, i):
        d = partner(i)
        return remote(
            send_v.at[k, d], dst.at[me], page_send.at[k, i], page_recv.at[k, i], "store", d
        )

    run(1, stores, lambda i: want_copy(i).start())
    run(1, tps, lambda i: new_copy(i).start())
    row_id[...] = one_hot_rows(stack)
    got_own.wait()
    run(1, stores, lambda i: want_copy(i).wait())
    scalars = local_copy(got, got_s, 4)
    scalars.start()
    pool_copy.wait()
    scalars.wait()

    def pack_send(k, dst):
        def body(i):
            d = partner(i)
            send_v[k, d] = pool_v[got_s[d, 0, k]]
            page_copy(k, dst, i).start()
        return body

    run(1, stores, pack_send(0, pages_ref))
    run(1, last_near, pack_send(1, near_ref))
    run(last_near, stores, pack_send(1, far_ref))
    own = []
    for k, dst in enumerate((pages_ref, near_ref)):
        send_v[k, me] = pool_v[got_s[me, 0, k]]
        own.append(local_copy(send_v.at[k, me], dst.at[me], 5 + k))
        own[k].start()
    for copy in own:
        copy.wait()
    own_new.wait()
    plan_copy.wait()
    run(0, blocks, lambda i: q_copy(i).wait())
    run(1, tps, lambda i: new_copy(i).wait())

    pages = plan.pages

    def first_mask(i):
        _, valid = plan.page(0, i // pages, i % pages)
        masks[i] = page_mask(0, valid - 1, 0)

    def second_mask(i):
        _, valid = plan.page(1, i // MIDDLE, i % MIDDLE)
        masks[requests * pages + i] = page_mask(0, valid - 1, 0)

    run(0, requests * pages, first_mask)
    run(0, requests * MIDDLE, second_mask)

    def stacked_rows(row0):
        return stacked(q_v[jnp.clip(row0 // ROWS, 0, blocks - 1)], row_id[...], heads)

    def save(item, acc, total, top):
        state[item, :, :HD] = acc
        state[item, :, HD:2 * HD] = total
        state[item, :, 2 * HD:] = top

    def new_item(item):
        r, row0, offset = plan.item(item)
        f0 = offset // PAGE
        new = (row0 + (ROWS - 1)) // PAGE + 1 - f0

        def place(i):
            return jnp.clip(f0 + i, 0, tps - 1)

        def key(i):
            base = PAGE * (f0 + i)
            low = jnp.where(i < new, offset - base, FAR)
            return [new_ref[place(i), 0], page_mask(low, row0 - base, 1)]

        count = 2 * ((MOST_NEW + PAGE - 2) // PAGE // 2 + 1)
        top, mixed = attend_pages(
            stacked_rows(row0),
            [functools.partial(key, i) for i in range(count)],
            [lambda i=i: new_ref[place(i), 1] for i in range(count)],
            scores, None,
        )
        save(item, mixed[:, :HD], mixed[:, HD:], top)

    def more(item, ref, group, first_mask_at, count):
        r, row0, _ = plan.item(item)

        def place(i):
            host, valid = plan.page(group, r, i)
            return jnp.clip(jnp.where(valid > 0, host, me), 0, stores - 1)

        acc = state[item, :, :HD]
        old = state[item, :, 2 * HD:]
        top, mixed = attend_pages(
            stacked_rows(row0),
            [lambda i=i: [ref[place(i), 0], masks[first_mask_at + r * count + i]] for i in range(count)],
            [lambda i=i: ref[place(i), 1] for i in range(count)],
            scores, old,
        )
        acc, total = merged(acc, state[item, :, HD:2 * HD], old, top, mixed)
        save(item, acc, total, top)

    run(0, items, new_item)
    run(1, stores, lambda i: page_copy(0, pages_ref, i).wait())
    run(0, items, lambda item: more(item, pages_ref, 0, 0, pages))
    run(1, last_near, lambda i: page_copy(1, near_ref, i).wait())
    run(0, items, lambda item: more(item, near_ref, 1, requests * pages, MIDDLE))
    run(last_near, stores, lambda i: page_copy(1, far_ref, i).wait())


def exchange(want, fresh_kv, page_pool, queries, requests, stores, tps):
    slots, _, page, width = page_pool.shape
    block_rows, columns = queries.shape
    heads = columns // HD
    dt = page_pool.dtype
    items = block_rows // ROWS + requests - 1
    stack = ROWS * heads
    vmem = pl.BlockSpec(memory_space=pltpu.VMEM)
    any_spec = pl.BlockSpec(memory_space=pl.ANY)
    sem = pltpu.SemaphoreType.DMA
    return pl.pallas_call(
        functools.partial(exchange_kernel, stores, tps, heads, requests),
        out_shape=(
            jax.ShapeDtypeStruct((stores, 2, page, width), dt),
            jax.ShapeDtypeStruct((stores, 2, page, width), dt),
            jax.ShapeDtypeStruct((items, stack, 3 * HD), jnp.float32),
        ),
        in_specs=[any_spec, any_spec, any_spec, any_spec],
        out_specs=(vmem, any_spec, vmem),
        scratch_shapes=[
            pltpu.VMEM((stores, 1, LANES), jnp.int32),
            pltpu.SMEM((stores, 1, LANES), jnp.int32),
            pltpu.SMEM((1, LANES), jnp.int32),
            pltpu.VMEM((tps, 2, page, width), dt),
            pltpu.VMEM((stores, 2, page, width), dt),
            pltpu.VMEM((slots, 2, page, width), dt),
            pltpu.VMEM((2, stores, 2, page, width), dt),
            pltpu.VMEM((block_rows // ROWS, ROWS, columns), dt),
            pltpu.VMEM((stack, HD), jnp.bfloat16),
            pltpu.VMEM((requests * (PAGES_MAX + MIDDLE), PAGE, HD), jnp.bfloat16),
            pltpu.VMEM((PAGES_MAX // 2, stack, 2 * PAGE), jnp.float32),
            sem((7,)),
            sem((block_rows // ROWS,)),
            sem((stores,)),
            sem((stores,)),
            sem((2, stores)),
            sem((2, stores)),
            sem((tps,)),
            sem((tps,)),
        ],
        compiler_params=pltpu.CompilerParams(
            collective_id=0, has_side_effects=True, vmem_limit_bytes=28 << 20
        ),
        name="exchange",
    )(want, fresh_kv, page_pool, queries)


def finish_kernel(
    heads, requests, plan_s, q_ref, state, near_ref, far_v, out_ref,
    out_v, row_id, scores, out_sem,
):
    own = lax.axis_index("store")
    stack = ROWS * heads
    blocks = out_v.shape[0]
    plan = Plan(lambda i: plan_s[i], requests, PAGES_MAX)
    def out_copy(b):
        return pltpu.make_async_copy(
            out_v.at[b], out_ref.at[pl.ds(pl.multiple_of(b * ROWS, ROWS), ROWS), :], out_sem.at[b]
        )

    row_id[...] = one_hot_rows(stack)
    out_row = lax.broadcasted_iota(jnp.int32, (ROWS, HD), 0)

    def one_request(r, carry):
        offset, item0 = carry
        length = plan.length(r)
        over = jnp.maximum(plan.size(1, r) - MIDDLE, 0)
        left = over + plan.size(2, r)
        b0 = offset // ROWS
        b1 = (offset + length - 1) // ROWS + 1

        def one_block(b, c):
            row0 = pl.multiple_of(b * ROWS, ROWS)
            item = item0 + b - b0
            mine = (out_row + row0 >= offset) & (out_row + row0 < offset + length)

            def page(i, half):
                is_near = i < over
                near_host, near_valid = plan.page(1, r, MIDDLE + i)
                far_host, far_valid = plan.page(2, r, i - over)
                use_near = is_near | (i >= left)
                data = jnp.where(
                    use_near,
                    near_ref[jnp.where(is_near, near_host, own), half],
                    far_v[jnp.where(use_near, 0, far_host), half],
                )
                valid = jnp.where(is_near, near_valid, jnp.where(i < left, far_valid, 0))
                return data, valid

            def key(i):
                k, valid = page(i, 0)
                return [k, page_mask(0, valid - 1, 0)]

            def variant(chunks):
                def body():
                    acc = state[item, :, :HD]
                    total = state[item, :, HD:2 * HD]
                    if chunks:
                        old = state[item, :, 2 * HD:]
                        q = stacked(q_ref[pl.ds(row0, ROWS), :], row_id[...], heads)
                        top, mixed = attend_pages(
                            q,
                            [functools.partial(key, i) for i in range(2 * chunks)],
                            [lambda i=i: page(i, 1)[0] for i in range(2 * chunks)],
                            scores, old,
                        )
                        acc, total = merged(acc, total, old, top, mixed)
                    result = (acc / total).astype(jnp.bfloat16)
                    for h in range(heads):
                        at = (b, slice(None), slice(h * HD, (h + 1) * HD))
                        out_v[at] = jnp.where(mine, result[h * ROWS:(h + 1) * ROWS], out_v[at])
                return body

            chunks = (left + 1) // 2
            for n in range(PAGES_MAX // 2 + 1):
                pl.when(chunks == n)(variant(n))

            @pl.when(offset + length >= row0 + ROWS)
            def _():
                out_copy(b).start()

            return c

        lax.fori_loop(b0, b1, one_block, 0)
        return offset + length, item0 + b1 - b0

    lax.fori_loop(0, requests, one_request, (0, 0))

    def wait_out(b, c):
        out_copy(b).wait()
        return c

    lax.fori_loop(0, blocks, wait_out, 0)


def finish(plan, queries, state, near, far, requests):
    block_rows, columns = queries.shape
    heads = columns // HD
    stack = ROWS * heads
    smem = pl.BlockSpec(memory_space=pltpu.SMEM)
    vmem = pl.BlockSpec(memory_space=pltpu.VMEM)
    any_spec = pl.BlockSpec(memory_space=pl.ANY)
    return pl.pallas_call(
        functools.partial(finish_kernel, heads, requests),
        out_shape=jax.ShapeDtypeStruct((block_rows, columns), queries.dtype),
        in_specs=[smem, vmem, vmem, vmem, vmem],
        out_specs=any_spec,
        scratch_shapes=[
            pltpu.VMEM((block_rows // ROWS, ROWS, columns), queries.dtype),
            pltpu.VMEM((stack, HD), jnp.bfloat16),
            pltpu.VMEM((PAGES_MAX // 2, stack, 2 * PAGE), jnp.float32),
            pltpu.SemaphoreType.DMA((block_rows // ROWS,)),
        ],
        compiler_params=pltpu.CompilerParams(vmem_limit_bytes=16 << 20),
        name="finish",
    )(plan, queries, state, near, far)


def in_hbm(x):
    return pltpu.with_memory_space_constraint(x, pltpu.HBM)


def local(queries, fresh_kv, page_pool, page_host, page_slot, prefix_len, fresh_len):
    stores = lax.axis_size("store")
    tps = lax.axis_size("tp")
    requests = page_host.shape[0]
    want, plan = make_plan(page_host, page_slot, prefix_len, fresh_len, stores)
    near, far, state = exchange(
        in_hbm(want), in_hbm(fresh_kv), in_hbm(page_pool), in_hbm(queries), requests, stores, tps
    )
    return finish(plan, queries, state, near, far, requests)


def solution(mesh):
    placed = (
        P("store", "tp"),
        P(None, ("store", "tp"), None),
        P("store", None, None, "tp"),
        P("store", None),
        P("store", None),
        P("store"),
        P("store", None),
    )
    return jax.shard_map(
        local, mesh=mesh, in_specs=placed, out_specs=P("store", "tp"), check_vma=False
    )
```

time: 141 us -> 126 us (0.89)
  Pallas kernels: 139 us -> 125 us
  local copies, waits for them, and re-layouts: 1.97 us -> 0.01 us
    pallas_call x3, Pallas kernels: 139 us -> 125 us  [the longest x1 112 us: exchange(): pl.pallas_call(functools.partial(exchange_kernel, stores, tps, heads, req...]
    unnamed x8 -> x4, local copies, waits for them, and re-layouts: 1.97 us -> 0.01 us
where the time goes in v4:
time: 126 us; the launch traced here: 125 us
  Pallas kernels  125 us (99%)
    pallas_call x1, Pallas kernels, exchange(): pl.pallas_call(functools.partial(exchange_kernel, stores, tps, heads, req...  112 us
    pallas_call x1, Pallas kernels, finish(): pl.pallas_call(functools.partial(finish_kernel, heads, requests), out_sha...  9.47 us
    pallas_call x1, Pallas kernels, make_plan(): pl.pallas_call(plan_kernel, out_shape=(jax.ShapeDtypeStruct((stores + 1,...  2.94 us

profile of v4, /device:TPU:40, one launch (start us, length us, event | category | flops | bytes accessed | tf_op | source)
XLA Modules:
  0.0 124.6 jit_solution(13143460616701102448)
XLA Ops:
  0.0 2.9 %plan.1 = (s32[33,1,128]{2,1,0:T(1,128)}, s32[128]{0:T(128)}) custom-call(s32[4,8]{1,0:T(4,128)} %host_s.1, s32[4,8]{1,0:T(4,128)} %slot_s.1, s32[4]{0:T(128)} %prefix_s.1, s32[1,4]{1,0:T(1,128)} %length_s.1), custom_call_target="tpu_custom_call" | custom-call | tf_op jit(solution)/shard_map/plan/pallas_call | solution.py:71
  2.9 0.0 copy-start
  3.0 0.0 copy-start.1
  3.0 112.1 %exchange.1 = (bf16[32,2,128,128]{3,2,1,0:T(8,128)(2,1)S(1)}, bf16[32,2,128,128]{3,2,1,0:T(8,128)(2,1)S(1)}, f32[19,512,384]{2,1,0:T(8,128)S(1)}) custom-call(s32[33,1,128]{2,1,0:T(1,128)} %get-tuple-element.11.want, bf16[2,128,1024]{2,1,0:T(8,128)(2,1)} %fresh_ref.1, bf16[64,2,128,128]{3,2,1,0:T(8,128)(2,1)} %pool_ref.1, bf16[1024,1024]{1,0:T(8,128)(2,1)} %q_ref.3), custom_call_target="tpu_custom_call" | custom-call | tf_op jit(solution)/shard_map/exchange/pallas_call | solution.py:370
  115.1 0.0 copy-done
  115.1 0.0 copy-done.1
  115.1 9.5 %finish.1 = bf16[1024,1024]{1,0:T(8,128)(2,1)} custom-call(s32[128]{0:T(128)S(1)} %copy-done.1, bf16[1024,1024]{1,0:T(8,128)(2,1)S(1)} %copy-done, f32[19,512,384]{2,1,0:T(8,128)S(1)} %get-tuple-element.12.state, bf16[32,2,128,128]{3,2,1,0:T(8,128)(2,1)S(1)} %get-tuple-element.13.near_ref, bf16[32,2,128,128]{3,2,1,0:T(8,128)(2,1)S(1)} %get-tuple-element.14.far_v), custom_call_target="tpu_custom_call" | custom-call | tf_op jit(solution)/shard_map/finish/pallas_call | solution.py:502
Async XLA Ops:
  2.9 112.2 %copy-start = (bf16[1024,1024]{1,0:T(8,128)(2,1)S(1)}, bf16[1024,1024]{1,0:T(8,128)(2,1)}, u32[]{:S(2)}) copy-start(bf16[1024,1024]{1,0:T(8,128)(2,1)} %q_ref.3) | copy-start | bytes 6291460
  3.0 112.2 %copy-start.1 = (s32[128]{0:T(128)S(1)}, s32[128]{0:T(128)}, u32[]{:S(2)}) copy-start(s32[128]{0:T(128)} %get-tuple-element.10.plan_s) | copy-start | bytes 1540

commit v5 on v4

--- a/solution.py
+++ b/solution.py
@@ -178,7 +178,7 @@
 def exchange_kernel(
     stores, tps, heads, requests, want, fresh_ref, pool_ref, q_ref,
     near_ref, far_ref, state,
-    got, got_s, plan_s, new_ref, pages_ref, pool_v, send_v, q_v, row_id, masks, scores,
+    got_s, plan_s, new_ref, pages_ref, pool_v, send_v, q_v, row_id, masks, scores,
     local_sem, q_sem, want_send, want_recv, page_send, page_recv, new_send, new_recv,
 ):
     me = lax.axis_index("store")
@@ -228,7 +228,7 @@
     own_new.start()
     plan_copy = local_copy(want.at[stores], plan_s, 2)
     plan_copy.start()
-    got_own = local_copy(want.at[me], got.at[me], 3)
+    got_own = local_copy(want.at[me], got_s.at[me], 3)
     got_own.start()
     run(0, blocks, lambda i: q_copy(i).start())
     pl.semaphore_wait(barrier, stores - 1 + tps - 1)
@@ -248,7 +248,7 @@
 
     def want_copy(i):
         d = partner(i)
-        return remote(want.at[d], got.at[me], want_send.at[i], want_recv.at[i], "store", d)
+        return remote(want.at[d], got_s.at[me], want_send.at[i], want_recv.at[i], "store", d)
 
     def page_copy(k, dst, i):
         d = partner(i)
@@ -261,10 +261,7 @@
     row_id[...] = one_hot_rows(stack)
     got_own.wait()
     run(1, stores, lambda i: want_copy(i).wait())
-    scalars = local_copy(got, got_s, 4)
-    scalars.start()
     pool_copy.wait()
-    scalars.wait()
 
     def pack_send(k, dst):
         def body(i):
@@ -377,7 +374,6 @@
         in_specs=[any_spec, any_spec, any_spec, any_spec],
         out_specs=(vmem, any_spec, vmem),
         scratch_shapes=[
-            pltpu.VMEM((stores, 1, LANES), jnp.int32),
             pltpu.SMEM((stores, 1, LANES), jnp.int32),
             pltpu.SMEM((1, LANES), jnp.int32),
             pltpu.VMEM((tps, 2, page, width), dt),

time: 126 us -> 125 us (level)
  no operation moved by 1% of the time
where the time goes in v5:
time: 125 us; the launch traced here: 124 us
  Pallas kernels  124 us (99%)
    pallas_call x1, Pallas kernels, exchange(): pl.pallas_call(functools.partial(exchange_kernel, stores, tps, heads, req...  111 us
    pallas_call x1, Pallas kernels, finish(): pl.pallas_call(functools.partial(finish_kernel, heads, requests), out_sha...  9.37 us
    pallas_call x1, Pallas kernels, make_plan(): pl.pallas_call(plan_kernel, out_shape=(jax.ShapeDtypeStruct((stores + 1,...  2.99 us

profile of v5, /device:TPU:40, one launch (start us, length us, event | category | flops | bytes accessed | tf_op | source)
XLA Modules:
  0.0 123.7 jit_solution(12101434302047125004)
XLA Ops:
  0.0 3.0 %plan.1 = (s32[33,1,128]{2,1,0:T(1,128)}, s32[128]{0:T(128)}) custom-call(s32[4,8]{1,0:T(4,128)} %host_s.1, s32[4,8]{1,0:T(4,128)} %slot_s.1, s32[4]{0:T(128)} %prefix_s.1, s32[1,4]{1,0:T(1,128)} %length_s.1), custom_call_target="tpu_custom_call" | custom-call | tf_op jit(solution)/shard_map/plan/pallas_call | solution.py:71
  3.0 0.0 copy-start
  3.0 0.0 copy-start.1
  3.0 111.3 %exchange.1 = (bf16[32,2,128,128]{3,2,1,0:T(8,128)(2,1)S(1)}, bf16[32,2,128,128]{3,2,1,0:T(8,128)(2,1)S(1)}, f32[19,512,384]{2,1,0:T(8,128)S(1)}) custom-call(s32[33,1,128]{2,1,0:T(1,128)} %get-tuple-element.11.want, bf16[2,128,1024]{2,1,0:T(8,128)(2,1)} %fresh_ref.1, bf16[64,2,128,128]{3,2,1,0:T(8,128)(2,1)} %pool_ref.1, bf16[1024,1024]{1,0:T(8,128)(2,1)} %q_ref.3), custom_call_target="tpu_custom_call" | custom-call | tf_op jit(solution)/shard_map/exchange/pallas_call | solution.py:367
  114.3 0.0 copy-done
  114.3 0.0 copy-done.1
  114.3 9.4 %finish.1 = bf16[1024,1024]{1,0:T(8,128)(2,1)} custom-call(s32[128]{0:T(128)S(1)} %copy-done.1, bf16[1024,1024]{1,0:T(8,128)(2,1)S(1)} %copy-done, f32[19,512,384]{2,1,0:T(8,128)S(1)} %get-tuple-element.12.state, bf16[32,2,128,128]{3,2,1,0:T(8,128)(2,1)S(1)} %get-tuple-element.13.near_ref, bf16[32,2,128,128]{3,2,1,0:T(8,128)(2,1)S(1)} %get-tuple-element.14.far_v), custom_call_target="tpu_custom_call" | custom-call | tf_op jit(solution)/shard_map/finish/pallas_call | solution.py:498
Async XLA Ops:
  3.0 111.3 %copy-start = (bf16[1024,1024]{1,0:T(8,128)(2,1)S(1)}, bf16[1024,1024]{1,0:T(8,128)(2,1)}, u32[]{:S(2)}) copy-start(bf16[1024,1024]{1,0:T(8,128)(2,1)} %q_ref.3) | copy-start | bytes 6291460
  3.0 111.3 %copy-start.1 = (s32[128]{0:T(128)S(1)}, s32[128]{0:T(128)}, u32[]{:S(2)}) copy-start(s32[128]{0:T(128)} %get-tuple-element.10.plan_s) | copy-start | bytes 1540
